TPU v7x, 32 devices: a whole 2x2x4 slice. The times are simulated.
32 devices in a mesh: groups: 2 (over x), role: 2 (over core), seq: 8 (over z, y).
Axes of the slice: x: 2, y: 2, z: 4, core: 2. Of those that a mesh axis runs over, the one named last changes fastest.
Arguments:
- kv_store: bfloat16 [2, 8192, 1024], P('role', ('groups', 'seq')), parts along dimension 1, may hold values from -6 to 6
- queries: bfloat16 [2, 256, 2, 4096], P('role', ('groups', 'seq')), parts along dimension 1, may hold values from -100 to 100
- step_kv: bfloat16 [256, 2, 1024], P(('groups', 'seq')), parts along dimension 0, may hold values from -6 to 6
- suffix_pages: int32 [256, 2], P(('groups', 'seq')), parts along dimension 0, may hold values from 0 to 31, as said below
- suffix_len: int32 [256], P(('groups', 'seq')), parts along dimension 0, may hold values from 2 to 32, as said below
- owner: int32 [256, 1], P(('groups', 'seq')), parts along dimension 0, may hold values from 0 to 7; in each aligned block of 16 rows (0 to 15, 16 to 31, ...) at most 4 rows name the same one
- parent_id: int32 [256], P(('groups', 'seq')), parts along dimension 0, may hold values from 0 to 1
- parent_pages: int32 [32, 16], P(('groups', 'seq')), parts along dimension 0, may hold values from 0 to 31, as said below
- parent_len: int32 [32], P(('groups', 'seq')), parts along dimension 0, may hold values from 1 to 256, as said below
Outputs:
- served: bfloat16 [2, 256, 2, 4096], P('role', ('groups', 'seq')), parts along dimension 1
There are 2 independent parts, one for each index of `groups`. A program takes and returns all parts, laid end to end along the dimension named above; each array names one. Nothing has to cross between parts.
Inputs may be any that keep to these rules, and one draw needn't show every extreme that they name: `suffix_pages`: on each device the page lists of its 16 requests are disjoint and together name every page of its store once. `suffix_len`: the first request of every device has the full 32 tokens. Of the requests of one device at most 4 go to one owner, and some device sends 4 to one owner. `parent_pages`: on each device the page tables of its 2 parent slots are disjoint and together name every page of its store once. `parent_len`: the first parent slot of every device has the full 256 tokens.
All inputs are finite; a program needn't handle non-finite values.
Results may differ from a plain program's by a relative error of at most 0.0025.
Values may be sent and summed in bfloat16 or wider, within the bound.
A program may use at most 128 MiB of HBM per device.

v0:
```python
import jax
import jax.numpy as jnp
from jax import lax
from jax.sharding import PartitionSpec as P

HEAD_DIM = 128
KV_HEADS = 4
GROUP = 8
PAGE = 16


MASKED_SCORE = -1e30


def as_sent(shard):

    def short(part):
        return part.astype(jnp.bfloat16) if part.dtype == jnp.float32 else part

    return jax.tree.map(short, shard)


def passed_along(block, axis, distance):
    devices = range(lax.axis_size(axis))
    route = [(i - distance, i) for i in devices if i - distance in devices]
    return lax.ppermute(block, axis, route)


def split_heads(kv_rows):
    key_width = KV_HEADS * HEAD_DIM
    shape_head = kv_rows.shape[:-1] + (KV_HEADS, HEAD_DIM)
    return (
        kv_rows[..., :key_width].reshape(shape_head),
        kv_rows[..., key_width:].reshape(shape_head),
    )


def prefill_rows(query_rows, suffix_kv, lengths):
    request_count = query_rows.shape[0]
    query_heads = query_rows.reshape(request_count, 2, KV_HEADS, GROUP, HEAD_DIM)
    key_rows, value_rows = split_heads(suffix_kv)
    scores = jnp.einsum(
        "rtgqh,rugh->rtgqu", query_heads, key_rows, preferred_element_type=jnp.float32
    ) * HEAD_DIM ** (-0.5)
    positions = jnp.arange(suffix_kv.shape[1])
    last_seen = lengths[:, None] - 2 + jnp.arange(2)[None, :]
    keep_mask = positions[None, None, :] <= last_seen[:, :, None]
    scores = jnp.where(keep_mask[:, :, None, None, :], scores, MASKED_SCORE)
    row_max = jnp.max(scores, axis=-1, keepdims=True)
    exp_terms = jnp.exp(scores - row_max)
    row_total = jnp.sum(exp_terms, axis=-1)
    blended = jnp.einsum(
        "rtgqu,rugh->rtgqh",
        exp_terms.astype(jnp.bfloat16),
        value_rows,
        preferred_element_type=jnp.float32,
    )
    return (blended / row_total[..., None]).astype(jnp.bfloat16).reshape(request_count, 2, -1)


def decode_rows(
    page_slots, query_slots, step_slots, meta_slots, parent_kv, parent_of, parent_pos, parent_cut
):
    slot_count = page_slots.shape[0]
    kv_width = parent_kv.shape[1]
    query_heads = query_slots.reshape(slot_count, 2, KV_HEADS, GROUP, HEAD_DIM)
    suffix_keys, suffix_values = split_heads(page_slots.reshape(slot_count, -1, kv_width))
    step_keys, step_values = split_heads(step_slots.reshape(slot_count, 2, kv_width))
    parent_keys, parent_values = split_heads(parent_kv)
    keep_parent = (parent_of[None, :] == meta_slots[:, 0:1]) & (
        parent_pos[None, :] < parent_cut[None, :]
    )
    keep_suffix = jnp.arange(suffix_keys.shape[1])[None, :] < meta_slots[:, 1:2]
    keep_step = jnp.arange(2)[None, :] <= jnp.arange(2)[:, None]
    scale = HEAD_DIM ** (-0.5)
    results = []
    for kv_head in range(KV_HEADS):
        query_one = query_heads[:, :, kv_head]
        score_parent = (
            jnp.einsum(
                "rtqh,ph->rtqp",
                query_one,
                parent_keys[:, kv_head],
                preferred_element_type=jnp.float32,
            )
            * scale
        )
        score_parent = jnp.where(keep_parent[:, None, None, :], score_parent, MASKED_SCORE)
        score_suffix = (
            jnp.einsum(
                "rtqh,ruh->rtqu",
                query_one,
                suffix_keys[:, :, kv_head],
                preferred_element_type=jnp.float32,
            )
            * scale
        )
        score_suffix = jnp.where(keep_suffix[:, None, None, :], score_suffix, MASKED_SCORE)
        score_step = (
            jnp.einsum(
                "rtqh,rnh->rtqn",
                query_one,
                step_keys[:, :, kv_head],
                preferred_element_type=jnp.float32,
            )
            * scale
        )
        score_step = jnp.where(keep_step[None, :, None, :], score_step, MASKED_SCORE)
        row_max = jnp.maximum(
            jnp.maximum(jnp.max(score_parent, axis=-1), jnp.max(score_suffix, axis=-1)),
            jnp.max(score_step, axis=-1),
        )[..., None]
        exp_parent = jnp.exp(score_parent - row_max)
        exp_suffix = jnp.exp(score_suffix - row_max)
        exp_step = jnp.exp(score_step - row_max)
        row_total = (
            jnp.sum(exp_parent, axis=-1) + jnp.sum(exp_suffix, axis=-1) + jnp.sum(exp_step, axis=-1)
        )
        blended = jnp.einsum(
            "rtqp,ph->rtqh",
            exp_parent.astype(jnp.bfloat16),
            parent_values[:, kv_head],
            preferred_element_type=jnp.float32,
        )
        blended = blended + jnp.einsum(
            "rtqu,ruh->rtqh",
            exp_suffix.astype(jnp.bfloat16),
            suffix_values[:, :, kv_head],
            preferred_element_type=jnp.float32,
        )
        blended = blended + jnp.einsum(
            "rtqn,rnh->rtqh",
            exp_step.astype(jnp.bfloat16),
            step_values[:, :, kv_head],
            preferred_element_type=jnp.float32,
        )
        results.append((blended / row_total[..., None]).astype(jnp.bfloat16))
    return jnp.stack(results, axis=2).reshape(slot_count, -1)


def pack_rows(pick_rows, row_values):
    return jnp.dot(
        pick_rows.astype(jnp.bfloat16), row_values, preferred_element_type=jnp.float32
    ).astype(jnp.bfloat16)


def local(
    kv_store, queries, step_kv, suffix_pages, suffix_len, owner, parent_id, parent_pages, parent_len
):
    role_index = lax.axis_index("role")
    seq_count = lax.axis_size("seq")
    page_store = kv_store[0]
    query_rows = queries[0]
    kv_width = page_store.shape[1]
    request_count = query_rows.shape[0]
    page_table = page_store.reshape(-1, PAGE * kv_width)
    suffix_flat = jnp.take(page_table, suffix_pages.reshape(-1), axis=0).reshape(request_count, -1)
    prefilled = prefill_rows(
        query_rows, suffix_flat.reshape(request_count, -1, kv_width), suffix_len
    )
    owner_col = owner[:, 0]
    ordinal = jnp.arange(request_count)
    earlier = (owner_col[:, None] == owner_col[None, :]) & (ordinal[None, :] < ordinal[:, None])
    slot_rank = jnp.sum(earlier, axis=1)
    capacity = max(2, 2 * request_count // seq_count)
    slot_total = seq_count * capacity
    placement = owner_col * capacity + slot_rank
    pick_rows = jnp.arange(slot_total)[:, None] == placement[None, :]
    meta_rows = jnp.stack([parent_id, suffix_len], axis=1)
    meta_slots = jnp.sum(
        jnp.where(pick_rows[:, :, None], meta_rows[None, :, :], 0), axis=1
    ).reshape(seq_count, capacity, 2)
    query_slots = pack_rows(pick_rows, query_rows.reshape(request_count, -1)).reshape(
        seq_count, capacity, -1
    )
    step_slots = pack_rows(pick_rows, step_kv.reshape(request_count, -1)).reshape(
        seq_count, capacity, -1
    )
    parent_kv = jnp.take(page_table, parent_pages.reshape(-1), axis=0).reshape(-1, kv_width)
    parent_span = parent_kv.shape[0] // parent_pages.shape[0]
    token_index = jnp.arange(parent_kv.shape[0])
    parent_of = token_index // parent_span
    parent_pos = token_index % parent_span
    parent_cut = jnp.sum(
        jnp.where(
            parent_of[:, None] == jnp.arange(parent_len.shape[0])[None, :], parent_len[None, :], 0
        ),
        axis=1,
    )
    page_slots = pack_rows(pick_rows, suffix_flat).reshape(seq_count, capacity, -1)
    page_width = page_slots.shape[2]
    query_width = query_slots.shape[2]
    step_width = step_slots.shape[2]
    combined = jnp.concatenate([query_slots, step_slots], axis=2)
    padded_rows = jnp.pad(combined, ((0, 0), (0, 0), (0, page_width - query_width - step_width)))
    payload = jnp.where(role_index == 0, page_slots, padded_rows)
    carried = lax.all_to_all(payload, "seq", split_axis=0, concat_axis=0, tiled=True)
    shifted = passed_along(carried, "role", 1)
    query_part = carried[:, :, :query_width]
    step_part = carried[:, :, query_width : query_width + step_width]
    serve_exchanged = (
        shifted,
        query_part,
        step_part,
        lax.all_to_all(meta_slots, "seq", split_axis=0, concat_axis=0, tiled=True),
    )
    source_count = serve_exchanged[0].shape[0]
    item_count = serve_exchanged[0].shape[1]
    operands = tuple(
        (
            member.reshape((source_count * item_count,) + member.shape[2:])
            for member in serve_exchanged
        )
    )
    finished = lax.cond(
        role_index == 1,
        lambda inputs: decode_rows(
            inputs[0], inputs[1], inputs[2], inputs[3], parent_kv, parent_of, parent_pos, parent_cut
        ),
        lambda inputs: jnp.zeros((inputs[1].shape[0], inputs[1].shape[1]), jnp.bfloat16),
        operands,
    )
    finished = finished.reshape(source_count, item_count, -1)
    returned = lax.all_to_all(
        as_sent(finished), "seq", split_axis=0, concat_axis=0, tiled=True
    ).astype(finished.dtype)
    decoded = jnp.take(returned.reshape(slot_total, -1), placement, axis=0).reshape(
        request_count, 2, -1
    )
    served = jnp.where(role_index == 0, prefilled, decoded)
    return served[None]


def solution(mesh):
    in_specs = (
        P("role", ("groups", "seq"), None),
        P("role", ("groups", "seq"), None, None),
        P(("groups", "seq"), None, None),
        P(("groups", "seq"), None),
        P(("groups", "seq")),
        P(("groups", "seq"), None),
        P(("groups", "seq")),
        P(("groups", "seq"), None),
        P(("groups", "seq")),
    )
    out_specs = P("role", ("groups", "seq"), None, None)
    return jax.shard_map(local, mesh=mesh, in_specs=in_specs, out_specs=out_specs, check_vma=False)
```

profile of v0, /device:TPU:1, one launch (start us, length us, event | category | flops | bytes accessed | tf_op | source)
XLA Modules:
  0.0 139.7 jit_solution(12882593423701290201)
XLA Ops:
  0.0 0.8 copy.170
  1.0 0.9 convert_reduce_fusion
  1.9 0.6 copy-done.18
  2.5 0.7 multiply_add_fusion
  3.1 0.9 copy.261
  4.3 1.1 copy.260
  5.4 0.4 convolution_convert_fusion.1
  5.9 1.0 reshape.361
  6.8 0.5 reshape_squeeze.9
  7.4 1.2 gather_fusion.1
  8.8 0.5 reshape.359
  9.2 2.1 %convolution_convert_fusion = bf16[32,32768]{1,0:T(8,128)(2,1)} fusion(bf16[16,32768]{1,0:T(8,128)(2,1)S(1)} %reshape.359, s32[16]{0:T(128)S(1)} %multiply_add_fusion), kind=kOutput, calls=%fused_computation.157 | convolution fusion | flops 34603520 | bytes 3145792 | tf_op jit(solution)/shard_map/dot_general | solution.py:142
  11.3 4.2 %reshape.360 = bf16[8,4,32768]{2,1,0:T(4,128)(2,1)} reshape(bf16[32,32768]{1,0:T(8,128)(2,1)} %convolution_convert_fusion) | data formatting | bytes 4194304 | tf_op jit(solution)/shard_map/reshape | solution.py:190
  15.5 1.1 fusion.90
  16.6 53.5 %all_to_all.15 = bf16[8,4,32768]{2,1,0:T(4,128)(2,1)} all-to-all(bf16[8,4,32768]{2,1,0:T(4,128)(2,1)S(1)} %fusion.90), channel_id=1, replica_groups=mesh['groups'=2,'role'=2,'seq'=8] {'seq'}, dimensions={0} | all-to-all | bytes 4194304 | tf_op jit(solution)/shard_map/all_to_all | solution.py:197
  70.2 1.4 %collective-permute-start = (bf16[8,4,32768]{2,1,0:T(4,128)(2,1)}, bf16[8,4,32768]{2,1,0:T(4,128)(2,1)}, u32[]{:S(2)}, u32[]{:S(2)}) collective-permute-start(bf16[8,4,32768]{2,1,0:T(4,128)(2,1)} %all_to_all.15), channel_id=1, source_target_pairs={{0,8},{1,9},{2,10},{3,11},{4,12},{5,13},{6,14},{7,15},{16,24},{17,... | collective-permute-start | bytes 6291464 | tf_op jit(solution)/shard_map/ppermute | solution.py:26
  71.9 0.6 copy.175
  72.5 4.2 %all-to-all-start = ((s32[8,4,2]{1,2,0:T(2,128)}), s32[8,4,2]{1,2,0:T(2,128)S(1)}, u32[]{:S(2)}, u32[]{:S(2)}) async-start(s32[8,4,2]{1,2,0:T(2,128)} %copy.175), calls=%async_computation | async-start | bytes 16384 | tf_op jit(solution)/shard_map/all_to_all | solution.py:205
  76.6 0.5 reshape_reshape.21
  77.4 0.9 fusion.126
  78.4 0.9 reshape_squeeze.10
  79.3 1.2 gather_fusion.2
  80.5 0.9 reshape.356
  81.4 0.6 all-to-all-done
  82.0 1.0 broadcast_in_dim.230
  83.1 39.2 %conditional.1 = (bf16[32,8192]{1,0:T(8,128)(2,1)S(1)}) conditional(s32[]{:T(128)} %convert_element_type.125, () %tuple.45, (s32[512]{0:T(512)S(1)}, s32[8,4,2]{1,2,0:T(2,128)S(1)}, s32[512]{0:T(512)S(1)}, s32[512,1]{0,1:T(1,128)S(1)}, s32[512,2]{0,1:T(2,128)S(1)}, /*index=5*/s32[2]{0:T(128)S(1)}, bf16[8,4,32768]{2,1,0:T(4,128)(2,1)}, ...), branch_computations={%region_4.6_spmd, %region_5.32_spmd} | conditional | flops 582753408 | bytes 65777132 | solution.py:215
  83.1 3.3 %reshape_reshape.18 = bf16[32,32,1024]{2,1,0:T(8,128)(2,1)S(1)} reshape(bf16[8,4,32768]{2,1,0:T(4,128)(2,1)} %get-tuple-element.258) | data formatting | bytes 4194304 | tf_op jit(solution)/shard_map/cond/branch_1_fun/reshape;reshape | solution.py:67
  86.4 1.6 %fusion.107 = (bf16[32,32,512]{2,1,0:T(8,128)(2,1)}, bf16[32,32,512]{2,1,0:T(8,128)(2,1)}) fusion(bf16[32,32,1024]{2,1,0:T(8,128)(2,1)S(1)} %reshape_reshape.18), kind=kLoop, calls=%fused_computation.203 | loop fusion | bytes 4194304 | tf_op jit(solution)/shard_map/cond/branch_1_fun/slice | solution.py:34
  88.0 1.4 %reshape.338 = bf16[32,32,4,128]{3,2,1,0:T(4,128)(2,1)S(1)} reshape(bf16[32,32,512]{2,1,0:T(8,128)(2,1)} %get-tuple-element.292) | data formatting | bytes 2097152 | tf_op jit(solution)/shard_map/cond/branch_1_fun/reshape | solution.py:34
  89.5 1.2 broadcast_select_fusion
  90.7 1.6 %reshape.333 = bf16[512,1024]{1,0:T(8,128)(2,1)S(1)} reshape(bf16[32,16384]{1,0:T(8,128)(2,1)} %broadcast_select_fusion) | data formatting | bytes 2097152 | tf_op jit(solution)/shard_map/reshape | solution.py:179
  92.4 1.0 copy.143
  93.8 1.0 slice.204
  94.7 1.2 slice.197
  95.9 0.5 reshape_reshape.17
  96.9 0.7 fusion.112
  97.6 1.3 fusion.123
  98.9 1.3 fusion.117
  100.2 1.9 %fusion.120 = (f32[32,2,8]{2,1,0:T(2,128)}, f32[32,2,8,2]{2,3,1,0:T(2,128)S(1)}) fusion(bf16[32,2,1,128]{3,2,1,0:T(2,128)(2,1)S(1)} %get-tuple-element.312, bf16[32,2,4,8,128]{4,3,2,1,0:T(8,128)(2,1)S(1)} %reshape_reshape.17, pred[2,2]{1,0:T(4,128)(4,1)} %copy-done.21), kind=kOutput, calls=%fused_computation.216 | convolution fusion | flops 264704 | bytes 169988 | tf_op jit(solution)/shard_map/cond/branch_1_fun/rtqh,rnh->rtqn/dot_general | solution.py:100
  102.2 1.9 %fusion.114 = (f32[32,2,8]{2,1,0:T(2,128)}, f32[32,2,8,2]{2,3,1,0:T(2,128)S(1)}) fusion(bf16[32,2,1,128]{3,2,1,0:T(2,128)(2,1)S(1)} %get-tuple-element.313, bf16[32,2,4,8,128]{4,3,2,1,0:T(8,128)(2,1)S(1)} %reshape_reshape.17, pred[2,2]{1,0:T(4,128)(4,1)} %copy-done.21), kind=kOutput, calls=%fused_computation.210 | convolution fusion | flops 264704 | bytes 169988 | tf_op jit(solution)/shard_map/cond/branch_1_fun/rtqh,rnh->rtqn/dot_general | solution.py:100
  104.1 1.0 copy.138
  105.1 1.3 reshape.335
  106.5 2.3 %fusion.109 = (bf16[32,32,1,128]{3,2,1,0:T(2,128)(2,1)S(1)}, bf16[32,32,1,128]{3,2,1,0:T(2,128)(2,1)S(1)}, bf16[32,32,1,128]{3,2,1,0:T(2,128)(2,1)S(1)}, bf16[32,32,1,128]{3,2,1,0:T(2,128)(2,1)S(1)}) fusion(bf16[32,32,4,128]{3,2,1,0:T(4,128)(2,1)S(1)} %reshape.335), kind=kLoop, calls=%fused_computation.205 | loop fusion | bytes 2097152 | tf_op jit(solution)/shard_map/cond/branch_1_fun/slice | solution.py:93
  108.8 0.4 fusion.125
  109.2 0.4 fusion.119
  109.5 0.4 fusion.122
  109.9 0.4 fusion.116
  110.3 2.5 %fusion.108 = (bf16[32,32,1,128]{3,2,1,0:T(2,128)(2,1)S(1)}, bf16[32,32,1,128]{3,2,1,0:T(2,128)(2,1)S(1)}, bf16[32,32,1,128]{3,2,1,0:T(2,128)(2,1)S(1)}, bf16[32,32,1,128]{3,2,1,0:T(2,128)(2,1)S(1)}) fusion(bf16[32,32,4,128]{3,2,1,0:T(4,128)(2,1)S(1)} %reshape.338), kind=kLoop, calls=%fused_computation.204 | loop fusion | bytes 2097152 | tf_op jit(solution)/shard_map/cond/branch_1_fun/slice | solution.py:128
  112.9 0.4 fusion.118
  114.1 0.4 fusion.38
  115.0 0.4 fusion.121
  116.3 0.4 fusion.40
  117.2 0.4 fusion.124
  117.7 0.4 fusion.115
  118.9 0.4 fusion.36
  119.3 0.4 fusion.42
  122.4 1.0 reshape.365
  123.3 4.9 %all-to-all-start.2 = ((bf16[8,4,8192]{2,1,0:T(4,128)(2,1)}), bf16[8,4,8192]{2,1,0:T(4,128)(2,1)S(1)}, u32[]{:S(2)}, u32[]{:S(2)}) async-start(bf16[8,4,8192]{2,1,0:T(4,128)(2,1)} %reshape.365), calls=%async_computation.2 | async-start | bytes 1048576 | tf_op jit(solution)/shard_map/all_to_all | solution.py:224
  128.2 0.5 fusion.127
  128.9 0.5 fusion.97
  129.3 0.4 fusion.94
  130.0 7.3 %all-to-all-done.2 = bf16[8,4,8192]{2,1,0:T(4,128)(2,1)S(1)} async-done(((bf16[8,4,8192]{2,1,0:T(4,128)(2,1)}), bf16[8,4,8192]{2,1,0:T(4,128)(2,1)S(1)}, u32[]{:S(2)}, u32[]{:S(2)}) %all-to-all-start.2) | async-done | bytes 524320 | tf_op jit(solution)/shard_map/all_to_all | solution.py:224
  137.5 0.7 gather_fusion
  138.7 1.0 copy.178
  (121 shorter events, 9.0 us)
Async XLA Ops:
  0.0 6.8 %copy-start.4 = (bf16[1,512,1024]{2,1,0:T(8,128)(2,1)S(1)}, bf16[1,512,1024]{2,1,0:T(8,128)(2,1)}, u32[]{:S(2)}) copy-start(bf16[1,512,1024]{2,1,0:T(8,128)(2,1)} %param.13) | copy-start | bytes 3145732
  1.9 0.6 copy-start.18
  11.3 4.2 %copy-start.1 = (bf16[8,4,8192]{2,1,0:T(4,128)(2,1)S(1)}, bf16[8,4,8192]{2,1,0:T(4,128)(2,1)}, u32[]{:S(2)}) copy-start(bf16[8,4,8192]{2,1,0:T(4,128)(2,1)} %reshape.361) | copy-start | bytes 1572868
  16.6 55.0 %copy-start.15 = (s32[16]{0:T(128)S(1)}, s32[16]{0:T(128)}, u32[]{:S(2)}) copy-start(s32[16]{0:T(128)} %param.19) | copy-start | bytes 196
  16.6 55.0 %copy-start.16 = (s32[16]{0:T(128)S(1)}, s32[16]{0:T(128)}, u32[]{:S(2)}) copy-start(s32[16]{0:T(128)} %param.17) | copy-start | bytes 196
  70.2 7.0 %copy-start.20 = (s32[2,16]{1,0:T(2,128)S(1)}, s32[2,16]{1,0:T(2,128)}, u32[]{:S(2)}) copy-start(s32[2,16]{1,0:T(2,128)} %param.20) | copy-start | bytes 388
  70.2 11.8 %collective-permute-start = (bf16[8,4,32768]{2,1,0:T(4,128)(2,1)}, bf16[8,4,32768]{2,1,0:T(4,128)(2,1)}, u32[]{:S(2)}, u32[]{:S(2)}) collective-permute-start(bf16[8,4,32768]{2,1,0:T(4,128)(2,1)} %all_to_all.15), channel_id=1, source_target_pairs={{0,8},{1,9},{2,10},{3,11},{4,12},{5,13},{6,14},{7,15},{16,24},{17,... | collective-permute-start | bytes 6291464 | tf_op jit(solution)/shard_map/ppermute | solution.py:26
  72.5 9.5 %all-to-all-start = ((s32[8,4,2]{1,2,0:T(2,128)}), s32[8,4,2]{1,2,0:T(2,128)S(1)}, u32[]{:S(2)}, u32[]{:S(2)}) async-start(s32[8,4,2]{1,2,0:T(2,128)} %copy.175), calls=%async_computation | async-start | bytes 16384 | tf_op jit(solution)/shard_map/all_to_all | solution.py:205
  76.6 1.7 %copy-start.5 = (bf16[1,16,2,4096]{3,2,1,0:T(2,128)(2,1)S(1)}, bf16[1,16,2,4096]{3,2,1,0:T(2,128)(2,1)}, u32[]{:S(2)}) copy-start(bf16[1,16,2,4096]{3,2,1,0:T(2,128)(2,1)} %param.14) | copy-start | bytes 786436
  80.5 2.6 %copy-start.14 = (s32[2]{0:T(128)S(1)}, s32[2]{0:T(128)}, u32[]{:S(2)}) copy-start(s32[2]{0:T(128)} %param.21) | copy-start | bytes 28
  88.0 1.5 %copy-start = (bf16[32,16384]{1,0:T(8,128)(2,1)S(1)}, bf16[32,16384]{1,0:T(8,128)(2,1)}, u32[]{:S(2)}) copy-start(bf16[32,16384]{1,0:T(8,128)(2,1)} %get-tuple-element.281) | copy-start | bytes 3145732 | tf_op jit(solution)/shard_map/cond
  89.5 9.5 %copy-start.21 = (pred[2,2]{1,0:T(4,128)(4,1)}, pred[2,2]{1,0:T(4,128)(4,1)S(1)}, u32[]{:S(2)}) copy-start(pred[2,2]{1,0:T(4,128)(4,1)S(1)} %iota_compare_fusion.1) | copy-start | bytes 16 | tf_op jit(solution)/shard_map/cond
  110.3 2.6 %copy-start.3 = (bf16[512,512]{0,1:T(8,128)(2,1)S(1)}, bf16[512,512]{0,1:T(8,128)(2,1)}, u32[]{:S(2)}) copy-start(bf16[512,512]{0,1:T(8,128)(2,1)} %copy.138) | copy-start | bytes 1572868 | tf_op jit(solution)/shard_map/cond
  110.3 3.0 %copy-start.13 = (f32[32,2,8]{2,1,0:T(2,128)S(1)}, f32[32,2,8]{2,1,0:T(2,128)}, u32[]{:S(2)}) copy-start(f32[32,2,8]{2,1,0:T(2,128)} %get-tuple-element.322) | copy-start | bytes 6148 | tf_op jit(solution)/shard_map/cond
  112.8 1.3 copy-start.7
  113.3 1.2 copy-start.9
  114.7 0.8 copy-start.12
  116.9 0.8 copy-start.10
  117.2 0.9 copy-start.11
  122.3 5.9 %copy-start.6 = (bf16[16,32,4,128]{3,2,1,0:T(4,128)(2,1)S(1)}, bf16[16,32,4,128]{3,2,1,0:T(4,128)(2,1)}, u32[]{:S(2)}) copy-start(bf16[16,32,4,128]{3,2,1,0:T(4,128)(2,1)} %reshape.356) | copy-start | bytes 1572868
  122.3 5.9 %copy-start.8 = (bf16[16,2,4,8,128]{4,3,2,1,0:T(8,128)(2,1)S(1)}, bf16[16,2,4,8,128]{4,3,2,1,0:T(8,128)(2,1)}, u32[]{:S(2)}) copy-start(bf16[16,2,4,8,128]{4,3,2,1,0:T(8,128)(2,1)} %reshape_squeeze.10) | copy-start | bytes 786436
  122.3 6.4 %copy-start.2 = (bf16[16,32,512]{2,1,0:T(8,128)(2,1)S(1)}, bf16[16,32,512]{2,1,0:T(8,128)(2,1)}, u32[]{:S(2)}) copy-start(bf16[16,32,512]{2,1,0:T(8,128)(2,1)} %get-tuple-element.341) | copy-start | bytes 1572868
  123.3 14.0 %all-to-all-start.2 = ((bf16[8,4,8192]{2,1,0:T(4,128)(2,1)}), bf16[8,4,8192]{2,1,0:T(4,128)(2,1)S(1)}, u32[]{:S(2)}, u32[]{:S(2)}) async-start(bf16[8,4,8192]{2,1,0:T(4,128)(2,1)} %reshape.365), calls=%async_computation.2 | async-start | bytes 1048576 | tf_op jit(solution)/shard_map/all_to_all | solution.py:224
  129.3 0.7 copy-start.17
  129.3 0.7 copy-start.19
where the time goes:
time: 140 us
  blocking collectives  53.5 us (38%)
  local copies, waits for them, and re-layouts  41.4 us (30%)
  matrix products  16.8 us (12%)
  starting transfers between devices  10.4 us (7%)
  other arithmetic  8.64 us (6%)
  waiting for transfers between devices  7.88 us (6%)
    all_to_all x1, blocking collectives, local(): lax.all_to_all(payload, 'seq', split_axis=0, concat_axis=0, tiled=True)  53.5 us
    all_to_all x1, waiting for transfers between devices, local(): lax.all_to_all(as_sent(finished), 'seq', split_axis=0, concat_axis=0, til...  7.3 us
    dot_general x4, matrix products, decode_rows(): jnp.einsum('rtqh,rnh->rtqn', query_one, step_keys[:, :, kv_head], preferr...  6.47 us
    all_to_all x1, starting transfers between devices, local(): lax.all_to_all(as_sent(finished), 'seq', split_axis=0, concat_axis=0, til...  4.86 us
    all_to_all x1, starting transfers between devices, local(): lax.all_to_all(meta_slots, 'seq', split_axis=0, concat_axis=0, tiled=True)  4.16 us
    reshape x1, local copies, waits for them, and re-layouts, local(): pack_rows(pick_rows, suffix_flat).reshape(seq_count, capacity, -1)  4.16 us
    unnamed x29, local copies, waits for them, and re-layouts  3.55 us
    another operation x1, local copies, waits for them, and re-layouts, decode_rows(): page_slots.reshape(slot_count, -1, kv_width)  3.27 us
  transfers between devices with their start and end apart: 3, of which 2 were waited for; matrix products, arithmetic and copies ran while one was open for 5% of the time, Pallas kernels for 0%

commit v1 on v0

v1 whole, which is shorter than its diff:
```python
import functools

import jax
import jax.numpy as jnp
from jax import lax
from jax.experimental import pallas as pl
from jax.experimental.pallas import tpu as pltpu
from jax.sharding import PartitionSpec as P

HEAD_DIM = 128
KV_HEADS = 4
GROUP = 8
PAGE = 16
LANES = 128
CHUNK = 64

MASKED_SCORE = -1e30
MESH = pl.DeviceIdType.MESH


def iota(shape, dim):
    return lax.broadcasted_iota(jnp.int32, shape, dim)


def spread(index, scalars):
    out = jnp.zeros(index.shape, jnp.int32)
    for i, scalar in enumerate(scalars):
        out = jnp.where(index == i, scalar, out)
    return out


def kernel(
    n_seq,
    cap,
    owner,
    parent_id,
    suffix_len,
    suffix_pages,
    parent_pages,
    parent_len,
    q_ref,
    kv_ref,
    step_ref,
    out_ref,
    slots,
    arrived,
    work,
    rows_meta,
    key_meta,
    full,
    stats,
    ret_send,
    ret_stat_send,
    ret,
    ret_stat,
    partner_q,
    partner_o,
    partner_stat,
    send_sem,
    recv_sem,
    osend_sem,
    orecv_sem,
    ssend_sem,
    srecv_sem,
    psend_sem,
    precv_sem,
):
    role = lax.axis_index("role")
    me = lax.axis_index("seq")
    requests = owner.shape[0]
    tokens, q_width = q_ref.shape
    per_peer = 2 * cap
    slot_rows = n_seq * per_peer
    key_count = kv_ref.shape[0]
    key_width = KV_HEADS * HEAD_DIM
    scale = HEAD_DIM ** (-0.5)
    partner = {"role": 1 - role}
    on_decode = role == 1
    on_prefill = role == 0

    def peer_at(step):
        return lax.rem(me + step, n_seq)

    barrier = pltpu.get_barrier_semaphore()
    pl.semaphore_signal(barrier, inc=1, device_id=partner, device_id_type=MESH)

    @pl.when(on_decode)
    def _():
        for step in range(1, n_seq):
            pl.semaphore_signal(
                barrier, inc=1, device_id={"seq": peer_at(step)}, device_id_type=MESH
            )
        pl.semaphore_wait(barrier, n_seq)

    @pl.when(on_prefill)
    def _():
        pl.semaphore_wait(barrier, 1)

    def remote(src, dst, ssem, rsem, device):
        return pltpu.make_async_remote_copy(
            src_ref=src,
            dst_ref=dst,
            send_sem=ssem,
            recv_sem=rsem,
            device_id=device,
            device_id_type=MESH,
        )

    q_to_partner = remote(q_ref, partner_q, psend_sem.at[0], precv_sem.at[0], partner)
    o_to_partner = remote(
        full.at[pl.ds(tokens, tokens)], partner_o, psend_sem.at[1], precv_sem.at[1], partner
    )
    s_to_partner = remote(
        stats.at[pl.ds(tokens, tokens)], partner_stat, psend_sem.at[2], precv_sem.at[2], partner
    )

    def slots_to(peer, mine):
        return remote(
            slots.at[peer], arrived.at[mine], send_sem.at[peer], recv_sem.at[mine], {"seq": peer}
        )

    def out_to(peer, mine):
        return remote(
            ret_send.at[peer], ret.at[mine], osend_sem.at[peer], orecv_sem.at[mine], {"seq": peer}
        )

    def stat_to(peer, mine):
        return remote(
            ret_stat_send.at[peer],
            ret_stat.at[mine],
            ssend_sem.at[peer],
            srecv_sem.at[mine],
            {"seq": peer},
        )

    owners = [owner[r, 0] for r in range(requests)]
    places = []
    for r in range(requests):
        rank = jnp.int32(0)
        for e in range(r):
            rank = rank + jnp.where(owners[e] == owners[r], 1, 0)
        places.append(owners[r] * cap + rank)
    lengths = [suffix_len[r] for r in range(requests)]
    parents = [parent_id[r] for r in range(requests)]

    @pl.when(on_decode)
    def _():
        q_to_partner.start()
        col = iota((1, tokens), 1)
        target = 2 * spread(col >> 1, places) + (col & 1)
        pick = jnp.where(iota((slot_rows, tokens), 0) == target, 1.0, 0.0).astype(jnp.bfloat16)
        tok = iota((tokens, LANES), 0) >> 1
        pid = spread(tok, parents).astype(jnp.float32).astype(jnp.bfloat16)
        pid_slots = jnp.dot(pick, pid, preferred_element_type=jnp.float32)
        for d in range(n_seq):
            slots[d, :, q_width:] = pid_slots[d * per_peer : (d + 1) * per_peer].astype(
                jnp.bfloat16
            )
        block = 8 * LANES
        for c in range(q_width // block):
            part = jnp.dot(
                pick, q_ref[:, c * block : (c + 1) * block], preferred_element_type=jnp.float32
            )
            for d in range(n_seq):
                slots[d, :, c * block : (c + 1) * block] = part[
                    d * per_peer : (d + 1) * per_peer
                ].astype(jnp.bfloat16)
        for step in range(1, n_seq):
            slots_to(peer_at(step), me).start()

    lane_page = iota((1, key_count), 1) // PAGE
    group_row = jnp.zeros((1, key_count), jnp.int32)
    base_row = jnp.zeros((1, key_count), jnp.int32)
    suf_pages = suffix_pages.shape[1]
    par_pages = parent_pages.shape[1]
    for j in range(key_count // PAGE):
        page = jnp.where(
            on_prefill,
            suffix_pages[j // suf_pages, j % suf_pages],
            parent_pages[j // par_pages, j % par_pages],
        )
        here = lane_page == page
        group_row = jnp.where(here, jnp.where(on_prefill, j // suf_pages, j // par_pages), group_row)
        base_row = jnp.where(
            here, jnp.where(on_prefill, j % suf_pages, j % par_pages) * PAGE, base_row
        )
    pos_row = base_row + (iota((1, key_count), 1) & (PAGE - 1))
    key_meta[0:1, :] = group_row
    key_meta[1:2, :] = pos_row

    @pl.when(on_prefill)
    def _():
        row = iota((2 * tokens, LANES), 0)
        late = row >= tokens
        request = jnp.where(late, row - tokens, row) >> 1
        turn = row & 1
        length = spread(request, lengths)
        rows_meta[0, 0 : 2 * tokens] = request
        rows_meta[1, 0 : 2 * tokens] = jnp.where(late, length, length - 1 + turn)
        rows_meta[2, 0 : 2 * tokens] = jnp.where(late, turn + 1, 0)
        work[0:tokens] = q_ref[...].astype(jnp.float32)
        q_to_partner.wait_recv()
        work[tokens : 2 * tokens] = partner_q[...].astype(jnp.float32)

    @pl.when(on_decode)
    def _():
        arrived[pl.ds(me, 1)] = slots[pl.ds(me, 1)]
        for step in range(1, n_seq):
            slots_to(me, peer_at(step)).wait_recv()
        cut = [parent_len[a] for a in range(parent_len.shape[0])]
        for s in range(n_seq):
            rows = slice(s * per_peer, (s + 1) * per_peer)
            work[rows, :] = arrived[s, :, :q_width].astype(jnp.float32)
            group = arrived[s, :, q_width:].astype(jnp.float32).astype(jnp.int32)
            rows_meta[0, rows] = group
            rows_meta[1, rows] = spread(group, cut)
            rows_meta[2, rows] = jnp.zeros_like(group)

    def attend(c):
        first = c * CHUNK
        if not isinstance(c, int):
            first = pl.multiple_of(first, CHUNK)
        rows = pl.ds(first, CHUNK)
        group = rows_meta[0, rows][:, 0:1]
        limit = rows_meta[1, rows][:, 0:1]
        step_limit = rows_meta[2, rows][:, 0:1]
        keep = (key_meta[0:1, :] == group) & (key_meta[1:2, :] < limit)
        bias = jnp.where(keep, 0.0, MASKED_SCORE)
        step_key = iota((CHUNK, tokens), 1)
        step_keep = ((step_key >> 1) == group) & ((step_key & 1) < step_limit)
        step_bias = jnp.where(step_keep, 0.0, MASKED_SCORE)
        bias = jnp.concatenate([bias] * GROUP, axis=0)
        step_bias = jnp.concatenate([step_bias] * GROUP, axis=0)
        lane = iota((CHUNK, LANES), 1)
        top_all = jnp.zeros((CHUNK, LANES), jnp.float32)
        sum_all = jnp.zeros((CHUNK, LANES), jnp.float32)
        for g in range(KV_HEADS):
            heads = [
                work[rows, (g * GROUP + h) * HEAD_DIM : (g * GROUP + h + 1) * HEAD_DIM].astype(
                    jnp.bfloat16
                )
                for h in range(GROUP)
            ]
            query = jnp.concatenate(heads, axis=0)
            ks = slice(g * HEAD_DIM, (g + 1) * HEAD_DIM)
            vs = slice(key_width + g * HEAD_DIM, key_width + (g + 1) * HEAD_DIM)
            contract = (((1,), (1,)), ((), ()))
            score = (
                lax.dot_general(
                    query, kv_ref[:, ks], contract, preferred_element_type=jnp.float32
                )
                * scale
                + bias
            )
            step_score = (
                lax.dot_general(
                    query, step_ref[:, ks], contract, preferred_element_type=jnp.float32
                )
                * scale
                + step_bias
            )
            top = jnp.maximum(
                jnp.max(score, axis=1, keepdims=True), jnp.max(step_score, axis=1, keepdims=True)
            )
            term = jnp.exp(score - top)
            step_term = jnp.exp(step_score - top)
            total = jnp.sum(term, axis=1, keepdims=True) + jnp.sum(
                step_term, axis=1, keepdims=True
            )
            mixed = jnp.dot(
                term.astype(jnp.bfloat16), kv_ref[:, vs], preferred_element_type=jnp.float32
            ) + jnp.dot(
                step_term.astype(jnp.bfloat16), step_ref[:, vs], preferred_element_type=jnp.float32
            )
            mixed = mixed / total
            for h in range(GROUP):
                head = g * GROUP + h
                part = slice(h * CHUNK, (h + 1) * CHUNK)
                full[rows, head * HEAD_DIM : (head + 1) * HEAD_DIM] = mixed[part]
                top_all = jnp.where(lane == head, top[part], top_all)
                sum_all = jnp.where(lane == head, total[part], sum_all)
        stats[rows, 0:LANES] = top_all
        stats[rows, LANES:] = sum_all

    chunks = work.shape[0] // CHUNK
    if chunks == 1:
        attend(0)
    else:

        def some(c, carry):
            attend(c)
            return carry

        lax.fori_loop(
            0, jnp.where(on_prefill, pl.cdiv(2 * tokens, CHUNK), slot_rows // CHUNK), some, 0
        )

    @pl.when(on_prefill)
    def _():
        o_to_partner.start()
        s_to_partner.start()
        out_ref[...] = full[0:tokens].astype(jnp.bfloat16)
        o_to_partner.wait_send()
        s_to_partner.wait_send()

    @pl.when(on_decode)
    def _():
        for s in range(n_seq):
            rows = slice(s * per_peer, (s + 1) * per_peer)
            ret_send[s] = full[rows].astype(jnp.bfloat16)
            ret_stat_send[s] = stats[rows]
        for step in range(1, n_seq):
            peer = peer_at(step)
            stat_to(peer, me).start()
            out_to(peer, me).start()
        ret[pl.ds(me, 1)] = ret_send[pl.ds(me, 1)]
        ret_stat[pl.ds(me, 1)] = ret_stat_send[pl.ds(me, 1)]
        tok = iota((tokens, 1), 0)
        target = 2 * spread(tok >> 1, places) + (tok & 1)
        unpick = jnp.where(iota((tokens, slot_rows), 1) == target, 1.0, 0.0)
        o_to_partner.wait_recv()
        s_to_partner.wait_recv()
        for step in range(1, n_seq):
            stat_to(me, peer_at(step)).wait_recv()
            out_to(me, peer_at(step)).wait_recv()
        back = jnp.concatenate([ret_stat[s] for s in range(n_seq)], axis=0)
        far = jnp.dot(
            unpick, back, preferred_element_type=jnp.float32, precision=lax.Precision.HIGHEST
        )
        far_top, far_sum = far[:, :LANES], far[:, LANES:]
        near_top, near_sum = partner_stat[:, :LANES], partner_stat[:, LANES:]
        top = jnp.maximum(far_top, near_top)
        far_weight = far_sum * jnp.exp(far_top - top)
        near_weight = near_sum * jnp.exp(near_top - top)
        total = jnp.where(near_weight + far_weight == 0.0, 1.0, near_weight + far_weight)
        far_share = far_weight / total
        near_share = near_weight / total
        unpick = unpick.astype(jnp.bfloat16)
        for head in range(KV_HEADS * GROUP):
            part = slice(head * HEAD_DIM, (head + 1) * HEAD_DIM)
            came = jnp.concatenate(
                [ret[s, :, part].astype(jnp.float32) for s in range(n_seq)], axis=0
            ).astype(jnp.bfloat16)
            far_out = jnp.dot(unpick, came, preferred_element_type=jnp.float32)
            out_ref[:, part] = (
                far_out * far_share[:, head : head + 1]
                + partner_o[:, part] * near_share[:, head : head + 1]
            ).astype(jnp.bfloat16)
        q_to_partner.wait_send()
        for step in range(1, n_seq):
            peer = peer_at(step)
            slots_to(peer, me).wait_send()
            out_to(peer, me).wait_send()
            stat_to(peer, me).wait_send()


def local(
    kv_store, queries, step_kv, suffix_pages, suffix_len, owner, parent_id, parent_pages, parent_len
):
    n_seq = lax.axis_size("seq")
    page_store = kv_store[0]
    requests, turns, q_width = queries.shape[1:]
    tokens = requests * turns
    query_rows = queries.reshape(tokens, q_width)
    step_rows = step_kv.reshape(tokens, -1)
    cap = max(4, 2 * requests // n_seq)
    per_peer = 2 * cap
    slot_rows = n_seq * per_peer
    work_rows = max(2 * tokens, slot_rows)
    bf16, f32 = jnp.bfloat16, jnp.float32
    smem = pl.BlockSpec(memory_space=pltpu.SMEM)
    vmem = pl.BlockSpec(memory_space=pltpu.VMEM)
    dma = pltpu.SemaphoreType.DMA
    served = pl.pallas_call(
        functools.partial(kernel, n_seq, cap),
        out_shape=jax.ShapeDtypeStruct((tokens, q_width), bf16),
        in_specs=[smem] * 6 + [vmem] * 3,
        out_specs=vmem,
        scratch_shapes=[
            pltpu.VMEM((n_seq, per_peer, q_width + LANES), bf16),
            pltpu.VMEM((n_seq, per_peer, q_width + LANES), bf16),
            pltpu.VMEM((work_rows, q_width), f32),
            pltpu.VMEM((3, work_rows, LANES), jnp.int32),
            pltpu.VMEM((8, page_store.shape[0]), jnp.int32),
            pltpu.VMEM((work_rows, q_width), f32),
            pltpu.VMEM((work_rows, 2 * LANES), f32),
            pltpu.VMEM((n_seq, per_peer, q_width), bf16),
            pltpu.VMEM((n_seq, per_peer, 2 * LANES), f32),
            pltpu.VMEM((n_seq, per_peer, q_width), bf16),
            pltpu.VMEM((n_seq, per_peer, 2 * LANES), f32),
            pltpu.VMEM((tokens, q_width), bf16),
            pltpu.VMEM((tokens, q_width), f32),
            pltpu.VMEM((tokens, 2 * LANES), f32),
            dma((n_seq,)),
            dma((n_seq,)),
            dma((n_seq,)),
            dma((n_seq,)),
            dma((n_seq,)),
            dma((n_seq,)),
            dma((3,)),
            dma((3,)),
        ],
        compiler_params=pltpu.CompilerParams(
            collective_id=0, has_side_effects=True, vmem_limit_bytes=60 * 1024 * 1024
        ),
    )(
        owner,
        parent_id,
        suffix_len,
        suffix_pages,
        parent_pages,
        parent_len,
        query_rows,
        page_store,
        step_rows,
    )
    return served.reshape(1, requests, turns, q_width)


def solution(mesh):
    in_specs = (
        P("role", ("groups", "seq"), None),
        P("role", ("groups", "seq"), None, None),
        P(("groups", "seq"), None, None),
        P(("groups", "seq"), None),
        P(("groups", "seq")),
        P(("groups", "seq"), None),
        P(("groups", "seq")),
        P(("groups", "seq"), None),
        P(("groups", "seq")),
    )
    out_specs = P("role", ("groups", "seq"), None, None)
    return jax.shard_map(local, mesh=mesh, in_specs=in_specs, out_specs=out_specs, check_vma=False)
```

time: 140 us -> 31.3 us (0.22)
  the two profiles are of different devices: /device:TPU:1 before, /device:TPU:25 now
where the time goes in v1:
time: 31.3 us; the launch traced here: 31.1 us
  Pallas kernels  24 us (77%)
  local copies, waits for them, and re-layouts  7.11 us (23%)
    pallas_call x1, Pallas kernels, local(): pl.pallas_call(functools.partial(kernel, n_seq, cap), out_shape=jax.Shape...  24 us
    unnamed x6, local copies, waits for them, and re-layouts  2.03 us
    reshape x1, local copies, waits for them, and re-layouts, local(): return served.reshape(1, requests, turns, q_width)  1.83 us
    reshape x1, local copies, waits for them, and re-layouts, local(): query_rows = queries.reshape(tokens, q_width)  1.75 us
    reshape x1, local copies, waits for them, and re-layouts, local(): step_rows = step_kv.reshape(tokens, -1)  1.5 us

profile of v1, /device:TPU:25, one launch (start us, length us, event | category | flops | bytes accessed | tf_op | source)
XLA Modules:
  0.0 31.1 jit_solution(7230946321228864043)
XLA Ops:
  0.0 0.0 copy-start
  0.0 0.7 %copy-done = s32[16,2]{0,1:T(2,128)S(1)} copy-done((s32[16,2]{0,1:T(2,128)S(1)}, s32[16,2]{0,1:T(2,128)}, u32[]{:S(2)}) %copy-start) | copy-done | bytes 152
  0.7 0.0 copy-start.1
  0.7 0.7 %copy.11.suffix_pages = s32[16,2]{1,0:T(8,128)} copy(s32[16,2]{0,1:T(2,128)S(1)} %copy-done) | data formatting | bytes 256 | tf_op args[3]
  1.4 0.0 copy-done.1
  1.4 0.7 %copy.10.owner = s32[16,1]{1,0:T(8,128)} copy(s32[16,1]{0,1:T(1,128)S(1)} %copy-done.1) | data formatting | bytes 128 | tf_op args[5]
  2.0 1.5 %reshape.10.step_ref = bf16[32,1024]{1,0:T(8,128)(2,1)} reshape(bf16[16,2,1024]{2,1,0:T(2,128)(2,1)} %param.11) | data formatting | bytes 131072 | tf_op jit(solution)/shard_map/reshape | solution.py:365
  3.5 1.7 %reshape.9.q_ref = bf16[32,4096]{1,0:T(8,128)(2,1)} reshape(bf16[1,16,2,4096]{3,2,1,0:T(2,128)(2,1)} %param.10) | data formatting | bytes 524288 | tf_op jit(solution)/shard_map/reshape | solution.py:364
  5.3 24.0 %shard_map.91 = bf16[32,4096]{1,0:T(8,128)(2,1)} custom-call(s32[16,1]{1,0:T(8,128)} %copy.10.owner, s32[16]{0:T(128)} %parent_id.1, s32[16]{0:T(128)} %suffix_len.1, s32[16,2]{1,0:T(8,128)} %copy.11.suffix_pages, s32[2,16]{1,0:T(2,128)} %parent_pages.1, s32[2]{0:T(128)} %parent_len.1, bf16[32,4096]{1,0:T(8,128)(2,1)} %reshape.9.q_ref, ...), custom_call_target="tpu_custom_call" | custom-call | tf_op jit(solution)/shard_map/pallas_call | solution.py:374
  29.2 1.8 %reshape.11 = bf16[1,16,2,4096]{3,2,1,0:T(2,128)(2,1)} reshape(bf16[32,4096]{1,0:T(8,128)(2,1)} %shard_map.91) | data formatting | bytes 524288 | tf_op jit(solution)/shard_map/reshape | solution.py:417
Async XLA Ops:
  0.0 0.7 %copy-start = (s32[16,2]{0,1:T(2,128)S(1)}, s32[16,2]{0,1:T(2,128)}, u32[]{:S(2)}) copy-start(s32[16,2]{0,1:T(2,128)} %param.12) | copy-start | bytes 388
  0.7 0.7 %copy-start.1 = (s32[16,1]{0,1:T(1,128)S(1)}, s32[16,1]{0,1:T(1,128)}, u32[]{:S(2)}) copy-start(s32[16,1]{0,1:T(1,128)} %param.14) | copy-start | bytes 196

commit v2 on v1

v2 whole, which is shorter than its diff:
```python
import functools

import jax
import jax.numpy as jnp
from jax import lax
from jax.experimental import pallas as pl
from jax.experimental.pallas import tpu as pltpu
from jax.sharding import PartitionSpec as P

HEAD_DIM = 128
KV_HEADS = 4
GROUP = 8
PAGE = 16
LANES = 128

MASKED_SCORE = -1e30
MESH = pl.DeviceIdType.MESH


def iota(shape, dim):
    return lax.broadcasted_iota(jnp.int32, shape, dim)


def spread(index, scalars):
    out = jnp.zeros(index.shape, jnp.int32)
    for i, scalar in enumerate(scalars):
        out = jnp.where(index == i, scalar, out)
    return out


def kernel(
    n_seq,
    cap,
    owner,
    parent_id,
    suffix_len,
    suffix_pages,
    parent_pages,
    parent_len,
    q_hbm,
    kv_hbm,
    step_hbm,
    out_ref,
    q_ref,
    kv_ref,
    step_in,
    step_ref,
    slots,
    arrived,
    work,
    rows_meta,
    key_meta,
    full,
    stats,
    near_send,
    near_stat_send,
    ret_send,
    ret_stat_send,
    ret,
    ret_stat,
    partner_q,
    partner_o,
    partner_stat,
    load_sem,
    send_sem,
    recv_sem,
    osend_sem,
    orecv_sem,
    ssend_sem,
    srecv_sem,
    psend_sem,
    precv_sem,
):
    role = lax.axis_index("role")
    me = lax.axis_index("seq")
    requests, turns, q_width = q_ref.shape
    tokens = requests * turns
    per_peer = 2 * cap
    slot_rows = n_seq * per_peer
    chunk = 2 * per_peer
    chunk_requests = chunk // turns
    near_chunks = tokens // chunk
    key_count = kv_ref.shape[0]
    key_width = KV_HEADS * HEAD_DIM
    scale = HEAD_DIM ** (-0.5)
    partner = {"role": 1 - role}
    on_decode = role == 1
    on_prefill = role == 0
    heads_all = KV_HEADS * GROUP

    def peer_at(step):
        if n_seq & (n_seq - 1):
            return lax.rem(me + step, n_seq)
        peer = 0
        bit = 1
        while bit < n_seq:
            peer = peer + bit * (((me // bit) % 2 + (step // bit) % 2) % 2)
            bit *= 2
        return peer

    load_q = pltpu.make_async_copy(q_hbm, q_ref, load_sem.at[0])
    load_step = pltpu.make_async_copy(step_hbm, step_in, load_sem.at[1])
    load_kv = pltpu.make_async_copy(kv_hbm, kv_ref, load_sem.at[2])
    load_q.start()
    load_step.start()
    load_kv.start()

    barrier = pltpu.get_barrier_semaphore()
    pl.semaphore_signal(barrier, inc=1, device_id=partner, device_id_type=MESH)

    @pl.when(on_decode)
    def _():
        for step in range(1, n_seq):
            pl.semaphore_signal(
                barrier, inc=1, device_id={"seq": peer_at(step)}, device_id_type=MESH
            )

    def remote(src, dst, ssem, rsem, device):
        return pltpu.make_async_remote_copy(
            src_ref=src,
            dst_ref=dst,
            send_sem=ssem,
            recv_sem=rsem,
            device_id=device,
            device_id_type=MESH,
        )

    q_to_partner = remote(q_ref, partner_q, psend_sem.at[0], precv_sem.at[0], partner)
    o_to_partner = remote(near_send, partner_o, psend_sem.at[1], precv_sem.at[1], partner)
    s_to_partner = remote(near_stat_send, partner_stat, psend_sem.at[2], precv_sem.at[2], partner)

    def slots_to(peer, mine):
        return remote(
            slots.at[peer], arrived.at[mine], send_sem.at[peer], recv_sem.at[mine], {"seq": peer}
        )

    def out_to(peer, mine):
        return remote(
            ret_send.at[peer], ret.at[mine], osend_sem.at[peer], orecv_sem.at[mine], {"seq": peer}
        )

    def stat_to(peer, mine):
        return remote(
            ret_stat_send.at[peer],
            ret_stat.at[mine],
            ssend_sem.at[peer],
            srecv_sem.at[mine],
            {"seq": peer},
        )

    owners = [owner[r] for r in range(requests)]
    places = []
    for r in range(requests):
        rank = jnp.int32(0)
        for e in range(r):
            rank = rank + jnp.where(owners[e] == owners[r], 1, 0)
        places.append(owners[r] * cap + rank)
    lengths = [suffix_len[r] for r in range(requests)]
    parents = [parent_id[r] for r in range(requests)]

    load_q.wait()

    @pl.when(on_decode)
    def _():
        col = iota((1, tokens), 1)
        target = 2 * spread(col >> 1, places) + (col & 1)
        pick = jnp.where(iota((slot_rows, tokens), 0) == target, 1.0, 0.0).astype(jnp.bfloat16)
        tok = iota((tokens, LANES), 0) >> 1
        pid = spread(tok, parents).astype(jnp.float32).astype(jnp.bfloat16)
        pid_slots = jnp.dot(pick, pid, preferred_element_type=jnp.float32)
        for d in range(n_seq):
            slots[d, :, q_width:] = pid_slots[d * per_peer : (d + 1) * per_peer].astype(
                jnp.bfloat16
            )
        block = 4 * LANES
        for c in range(q_width // block):
            lanes = slice(c * block, (c + 1) * block)
            part = jnp.dot(
                pick, q_ref[:, :, lanes].reshape(tokens, block), preferred_element_type=jnp.float32
            )
            for d in range(n_seq):
                slots[d, :, lanes] = part[d * per_peer : (d + 1) * per_peer].astype(jnp.bfloat16)
        pl.semaphore_wait(barrier, n_seq)
        q_to_partner.start()
        for step in range(n_seq - 1, 0, -1):
            slots_to(peer_at(step), me).start()
        arrived[pl.ds(me, 1)] = slots[pl.ds(me, 1)]

    @pl.when(on_prefill)
    def _():
        pl.semaphore_wait(barrier, 1)

    lane_page = iota((1, key_count), 1) // PAGE
    group_row = jnp.zeros((1, key_count), jnp.int32)
    base_row = jnp.zeros((1, key_count), jnp.int32)
    suf_pages = suffix_pages.shape[0]
    par_pages = parent_pages.shape[1]
    for j in range(key_count // PAGE):
        page = jnp.where(
            on_prefill,
            suffix_pages[j % suf_pages, j // suf_pages],
            parent_pages[j // par_pages, j % par_pages],
        )
        here = lane_page == page
        group_row = jnp.where(here, jnp.where(on_prefill, j // suf_pages, j // par_pages), group_row)
        base_row = jnp.where(
            here, jnp.where(on_prefill, j % suf_pages, j % par_pages) * PAGE, base_row
        )
    pos_row = base_row + (iota((1, key_count), 1) & (PAGE - 1))
    key_meta[0:1, :] = group_row
    key_meta[1:2, :] = pos_row
    load_step.wait()
    for c in range(step_ref.shape[1] // (4 * LANES)):
        lanes = slice(c * 4 * LANES, (c + 1) * 4 * LANES)
        step_ref[:, lanes] = step_in[:, :, lanes].reshape(tokens, 4 * LANES)
    cuts = [parent_len[a] for a in range(parent_len.shape[0])]
    load_kv.wait()

    def attend():
        group = rows_meta[0, :, 0:1]
        limit = rows_meta[1, :, 0:1]
        step_limit = rows_meta[2, :, 0:1]
        keep = (key_meta[0:1, :] == group) & (key_meta[1:2, :] < limit)
        bias = jnp.where(keep, 0.0, MASKED_SCORE)
        step_key = iota((chunk, tokens), 1)
        step_keep = ((step_key >> 1) == group) & ((step_key & 1) < step_limit)
        step_bias = jnp.where(step_keep, 0.0, MASKED_SCORE)
        bias = jnp.concatenate([bias] * GROUP, axis=0)
        step_bias = jnp.concatenate([step_bias] * GROUP, axis=0)
        lane = iota((chunk, LANES), 1)
        top_all = jnp.zeros((chunk, LANES), jnp.float32)
        sum_all = jnp.zeros((chunk, LANES), jnp.float32)
        for g in range(KV_HEADS):
            query = jnp.concatenate(
                [
                    work[:, (g * GROUP + h) * HEAD_DIM : (g * GROUP + h + 1) * HEAD_DIM]
                    for h in range(GROUP)
                ],
                axis=0,
            )
            ks = slice(g * HEAD_DIM, (g + 1) * HEAD_DIM)
            vs = slice(key_width + g * HEAD_DIM, key_width + (g + 1) * HEAD_DIM)
            contract = (((1,), (1,)), ((), ()))
            score = (
                lax.dot_general(
                    query, kv_ref[:, ks], contract, preferred_element_type=jnp.float32
                )
                * scale
                + bias
            )
            step_score = (
                lax.dot_general(
                    query, step_ref[:, ks], contract, preferred_element_type=jnp.float32
                )
                * scale
                + step_bias
            )
            top = jnp.maximum(
                jnp.max(score, axis=1, keepdims=True), jnp.max(step_score, axis=1, keepdims=True)
            )
            term = jnp.exp(score - top)
            step_term = jnp.exp(step_score - top)
            total = jnp.sum(term, axis=1, keepdims=True) + jnp.sum(
                step_term, axis=1, keepdims=True
            )
            mixed = jnp.dot(
                term.astype(jnp.bfloat16), kv_ref[:, vs], preferred_element_type=jnp.float32
            ) + jnp.dot(
                step_term.astype(jnp.bfloat16), step_ref[:, vs], preferred_element_type=jnp.float32
            )
            mixed = mixed / total
            for h in range(GROUP):
                head = g * GROUP + h
                part = slice(h * chunk, (h + 1) * chunk)
                full[:, head * HEAD_DIM : (head + 1) * HEAD_DIM] = mixed[part]
                top_all = jnp.where(lane == head, top[part], top_all)
                sum_all = jnp.where(lane == head, total[part], sum_all)
        stats[:, 0:LANES] = top_all
        stats[:, LANES:] = sum_all

    def turn_of(c, carry):
        late = c >= near_chunks
        block = jnp.where(late, c - near_chunks, c)
        first_request = block * chunk_requests
        steps = (n_seq - 1 - 2 * c, n_seq - 2 - 2 * c)

        @pl.when(on_prefill)
        def _():
            row = iota((chunk, LANES), 0)
            request = first_request + (row >> 1)
            turn = row & 1
            length = spread(request, lengths)
            rows_meta[0] = request
            rows_meta[1] = jnp.where(late, length, length - 1 + turn)
            rows_meta[2] = jnp.where(late, turn + 1, 0)

            @pl.when(c == near_chunks)
            def _():
                q_to_partner.wait_recv()

            @pl.when(late)
            def _():
                for h in range(heads_all):
                    part = slice(h * HEAD_DIM, (h + 1) * HEAD_DIM)
                    work[:, part] = partner_q[
                        pl.ds(first_request, chunk_requests), :, part
                    ].reshape(chunk, HEAD_DIM)

            @pl.when(jnp.logical_not(late))
            def _():
                for h in range(heads_all):
                    part = slice(h * HEAD_DIM, (h + 1) * HEAD_DIM)
                    work[:, part] = q_ref[pl.ds(first_request, chunk_requests), :, part].reshape(
                        chunk, HEAD_DIM
                    )

        @pl.when(on_decode)
        def _():
            for i, step in enumerate(steps):
                peer = peer_at(step)

                @pl.when(step > 0)
                def _():
                    slots_to(me, peer).wait_recv()

            first, second = peer_at(steps[0]), peer_at(steps[1])
            for h in range(heads_all):
                part = slice(h * HEAD_DIM, (h + 1) * HEAD_DIM)
                work[:, part] = jnp.concatenate(
                    [
                        arrived[first, :, part].astype(jnp.float32),
                        arrived[second, :, part].astype(jnp.float32),
                    ],
                    axis=0,
                ).astype(jnp.bfloat16)
            group = jnp.concatenate(
                [
                    arrived[first, :, q_width:].astype(jnp.float32),
                    arrived[second, :, q_width:].astype(jnp.float32),
                ],
                axis=0,
            ).astype(jnp.int32)
            rows_meta[0] = group
            rows_meta[1] = spread(group, cuts)
            rows_meta[2] = jnp.zeros_like(group)

        attend()

        @pl.when(on_prefill)
        def _():
            @pl.when(late)
            def _():
                rows = pl.ds(pl.multiple_of(block * chunk, chunk), chunk)
                near_send[rows, :] = full[...]
                near_stat_send[rows, :] = stats[...]

            @pl.when(jnp.logical_not(late))
            def _():
                for h in range(heads_all):
                    part = slice(h * HEAD_DIM, (h + 1) * HEAD_DIM)
                    out_ref[pl.ds(first_request, chunk_requests), :, part] = (
                        full[:, part].astype(jnp.bfloat16).reshape(chunk_requests, turns, HEAD_DIM)
                    )

        @pl.when(on_decode)
        def _():
            for i, step in enumerate(steps):
                peer = peer_at(step)
                rows = slice(i * per_peer, (i + 1) * per_peer)
                ret_send[peer] = full[rows].astype(jnp.bfloat16)
                ret_stat_send[peer] = stats[rows]

                @pl.when(step > 0)
                def _():
                    stat_to(peer, me).start()
                    out_to(peer, me).start()

        return carry

    lax.fori_loop(0, jnp.where(on_prefill, 2 * near_chunks, n_seq // 2), turn_of, 0)

    @pl.when(on_prefill)
    def _():
        s_to_partner.start()
        o_to_partner.start()
        s_to_partner.wait_send()
        o_to_partner.wait_send()

    @pl.when(on_decode)
    def _():
        ret[pl.ds(me, 1)] = ret_send[pl.ds(me, 1)]
        ret_stat[pl.ds(me, 1)] = ret_stat_send[pl.ds(me, 1)]
        tok = iota((tokens, 1), 0)
        target = 2 * spread(tok >> 1, places) + (tok & 1)
        unpick = jnp.where(iota((tokens, slot_rows), 1) == target, 1.0, 0.0)
        o_to_partner.wait_recv()
        s_to_partner.wait_recv()
        for step in range(n_seq - 1, 0, -1):
            stat_to(me, peer_at(step)).wait_recv()
            out_to(me, peer_at(step)).wait_recv()
        back = jnp.concatenate([ret_stat[s] for s in range(n_seq)], axis=0)
        far = jnp.dot(
            unpick, back, preferred_element_type=jnp.float32, precision=lax.Precision.HIGHEST
        )
        far_top, far_sum = far[:, :LANES], far[:, LANES:]
        near_top, near_sum = partner_stat[:, :LANES], partner_stat[:, LANES:]
        top = jnp.maximum(far_top, near_top)
        far_weight = far_sum * jnp.exp(far_top - top)
        near_weight = near_sum * jnp.exp(near_top - top)
        total = jnp.where(near_weight + far_weight == 0.0, 1.0, near_weight + far_weight)
        far_share = far_weight / total
        near_share = near_weight / total
        unpick = unpick.astype(jnp.bfloat16)
        for head in range(heads_all):
            part = slice(head * HEAD_DIM, (head + 1) * HEAD_DIM)
            came = jnp.concatenate(
                [ret[s, :, part].astype(jnp.float32) for s in range(n_seq)], axis=0
            ).astype(jnp.bfloat16)
            far_out = jnp.dot(unpick, came, preferred_element_type=jnp.float32)
            out_ref[:, :, part] = (
                (
                    far_out * far_share[:, head : head + 1]
                    + partner_o[:, part] * near_share[:, head : head + 1]
                )
                .astype(jnp.bfloat16)
                .reshape(requests, turns, HEAD_DIM)
            )
        q_to_partner.wait_send()
        for step in range(1, n_seq):
            peer = peer_at(step)
            slots_to(peer, me).wait_send()
            out_to(peer, me).wait_send()
            stat_to(peer, me).wait_send()


def local(
    kv_store, queries, step_kv, suffix_pages, suffix_len, owner, parent_id, parent_pages, parent_len
):
    n_seq = lax.axis_size("seq")
    page_store = kv_store[0]
    requests, turns, q_width = queries.shape[1:]
    tokens = requests * turns
    cap = max(4, 2 * requests // n_seq)
    per_peer = 2 * cap
    chunk = 2 * per_peer
    bf16, f32 = jnp.bfloat16, jnp.float32
    smem = pl.BlockSpec(memory_space=pltpu.SMEM)
    vmem = pl.BlockSpec(memory_space=pltpu.VMEM)
    hbm = pl.BlockSpec(memory_space=pl.ANY)
    dma = pltpu.SemaphoreType.DMA
    served = pl.pallas_call(
        functools.partial(kernel, n_seq, cap),
        out_shape=jax.ShapeDtypeStruct((requests, turns, q_width), bf16),
        in_specs=[smem] * 6 + [hbm] * 3,
        out_specs=vmem,
        scratch_shapes=[
            pltpu.VMEM((requests, turns, q_width), bf16),
            pltpu.VMEM(page_store.shape, bf16),
            pltpu.VMEM(step_kv.shape, bf16),
            pltpu.VMEM((tokens, step_kv.shape[2]), bf16),
            pltpu.VMEM((n_seq, per_peer, q_width + LANES), bf16),
            pltpu.VMEM((n_seq, per_peer, q_width + LANES), bf16),
            pltpu.VMEM((chunk, q_width), bf16),
            pltpu.VMEM((3, chunk, LANES), jnp.int32),
            pltpu.VMEM((8, page_store.shape[0]), jnp.int32),
            pltpu.VMEM((chunk, q_width), f32),
            pltpu.VMEM((chunk, 2 * LANES), f32),
            pltpu.VMEM((tokens, q_width), f32),
            pltpu.VMEM((tokens, 2 * LANES), f32),
            pltpu.VMEM((n_seq, per_peer, q_width), bf16),
            pltpu.VMEM((n_seq, per_peer, 2 * LANES), f32),
            pltpu.VMEM((n_seq, per_peer, q_width), bf16),
            pltpu.VMEM((n_seq, per_peer, 2 * LANES), f32),
            pltpu.VMEM((requests, turns, q_width), bf16),
            pltpu.VMEM((tokens, q_width), f32),
            pltpu.VMEM((tokens, 2 * LANES), f32),
            dma((3,)),
            dma((n_seq,)),
            dma((n_seq,)),
            dma((n_seq,)),
            dma((n_seq,)),
            dma((n_seq,)),
            dma((n_seq,)),
            dma((3,)),
            dma((3,)),
        ],
        compiler_params=pltpu.CompilerParams(
            collective_id=0, has_side_effects=True, vmem_limit_bytes=60 * 1024 * 1024
        ),
    )(
        owner.reshape(-1),
        parent_id,
        suffix_len,
        suffix_pages.T,
        parent_pages,
        parent_len,
        queries[0],
        page_store,
        step_kv,
    )
    return served[None]


def solution(mesh):
    in_specs = (
        P("role", ("groups", "seq"), None),
        P("role", ("groups", "seq"), None, None),
        P(("groups", "seq"), None, None),
        P(("groups", "seq"), None),
        P(("groups", "seq")),
        P(("groups", "seq"), None),
        P(("groups", "seq")),
        P(("groups", "seq"), None),
        P(("groups", "seq")),
    )
    out_specs = P("role", ("groups", "seq"), None, None)
    return jax.shard_map(local, mesh=mesh, in_specs=in_specs, out_specs=out_specs, check_vma=False)
```

time: 31.3 us -> 24.4 us (0.78)
  the two profiles are of different devices: /device:TPU:25 before, /device:TPU:1 now
where the time goes in v2:
time: 24.4 us; the launch traced here: 24.2 us
  Pallas kernels  22.3 us (91%)
  local copies, waits for them, and re-layouts  1.85 us (8%)
    pallas_call x1, Pallas kernels, local(): pl.pallas_call(functools.partial(kernel, n_seq, cap), out_shape=jax.Shape...  22.3 us
    unnamed x1, local copies, waits for them, and re-layouts  1.85 us

profile of v2, /device:TPU:1, one launch (start us, length us, event | category | flops | bytes accessed | tf_op | source)
XLA Modules:
  0.0 24.2 jit_solution(15195483181952404924)
XLA Ops:
  0.0 22.3 %shard_map.91 = bf16[16,2,4096]{2,1,0:T(2,128)(2,1)} custom-call(s32[16]{0:T(128)} %bitcast.9, s32[16]{0:T(128)} %parent_id.1, s32[16]{0:T(128)} %suffix_len.1, s32[2,16]{1,0:T(2,128)} %bitcast.8, s32[2,16]{1,0:T(2,128)} %parent_pages.1, s32[2]{0:T(128)} %parent_len.1, bf16[16,2,4096]{2,1,0:T(2,128)(2,1)} %bitcast.7, bf16[512,1024]{1,0:T(8,128)(2,1)} %bitcast.6, ...), custom_call_target="tpu_custom_call" | custom-call | tf_op jit(solution)/shard_map/pallas_call | solution.py:451
  22.3 1.9 %copy.11 = bf16[1,16,2,4096]{3,2,1,0:T(2,128)(2,1)} copy(bf16[1,16,2,4096]{3,2,1,0:T(2,128)(2,1)} %bitcast.5) | data formatting | bytes 524288

commit v3 on v2

v3 whole, which is shorter than its diff:
```python
import functools

import jax
import jax.numpy as jnp
from jax import lax
from jax.experimental import pallas as pl
from jax.experimental.pallas import tpu as pltpu
from jax.sharding import PartitionSpec as P

HEAD_DIM = 128
KV_HEADS = 4
GROUP = 8
PAGE = 16
LANES = 128

MASKED_SCORE = -1e30
MESH = pl.DeviceIdType.MESH


def iota(shape, dim):
    return lax.broadcasted_iota(jnp.int32, shape, dim)


def spread(index, scalars):
    out = jnp.zeros(index.shape, jnp.int32)
    for i, scalar in enumerate(scalars):
        out = jnp.where(index == i, scalar, out)
    return out


def kernel(
    n_seq,
    cap,
    owner_hbm,
    parent_id_hbm,
    suffix_len_hbm,
    suffix_pages_hbm,
    parent_pages_hbm,
    parent_len_hbm,
    q_hbm,
    kv_hbm,
    step_hbm,
    out_ref,
    owner,
    parent_id,
    suffix_len,
    suffix_pages,
    parent_pages,
    parent_len,
    q_ref,
    kv_ref,
    step_in,
    step_ref,
    slots,
    arrived,
    key_meta,
    near_send,
    near_stat_send,
    ret_send,
    ret_stat_send,
    ret,
    ret_stat,
    partner_q,
    partner_o,
    partner_stat,
    load_sem,
    send_sem,
    recv_sem,
    osend_sem,
    orecv_sem,
    ssend_sem,
    srecv_sem,
    psend_sem,
    precv_sem,
):
    role = lax.axis_index("role")
    me = lax.axis_index("seq")
    requests, turns, q_width = q_ref.shape
    tokens = requests * turns
    per_peer = 2 * cap
    slot_rows = n_seq * per_peer
    key_count = kv_ref.shape[0]
    key_width = KV_HEADS * HEAD_DIM
    scale = HEAD_DIM ** (-0.5)
    partner = {"role": 1 - role}
    on_decode = role == 1
    on_prefill = role == 0
    heads_all = KV_HEADS * GROUP

    bits = [(me // 2**b) % 2 for b in range(n_seq.bit_length() - 1)]

    def peer_at(step):
        if n_seq & (n_seq - 1):
            return lax.rem(me + step, n_seq)
        peer = me
        for b, mine in enumerate(bits):
            if isinstance(step, int):
                if (step >> b) & 1:
                    peer = peer + 2**b * (1 - 2 * mine)
            else:
                peer = peer + 2**b * (1 - 2 * mine) * ((step // 2**b) % 2)
        return peer

    load_q = pltpu.make_async_copy(q_hbm, q_ref, load_sem.at[0])
    load_step = pltpu.make_async_copy(step_hbm, step_in, load_sem.at[1])
    load_kv = pltpu.make_async_copy(kv_hbm, kv_ref, load_sem.at[2])
    tables = [
        pltpu.make_async_copy(src, dst, load_sem.at[3 + i])
        for i, (src, dst) in enumerate(
            (
                (owner_hbm, owner),
                (parent_id_hbm, parent_id),
                (suffix_len_hbm, suffix_len),
                (suffix_pages_hbm, suffix_pages),
                (parent_pages_hbm, parent_pages),
                (parent_len_hbm, parent_len),
            )
        )
    ]
    load_q.start()
    for table in tables:
        table.start()
    load_step.start()
    load_kv.start()

    barrier = pltpu.get_barrier_semaphore()
    pl.semaphore_signal(barrier, inc=1, device_id=partner, device_id_type=MESH)

    @pl.when(on_decode)
    def _():
        for step in range(1, n_seq):
            pl.semaphore_signal(
                barrier, inc=1, device_id={"seq": peer_at(step)}, device_id_type=MESH
            )

    def remote(src, dst, ssem, rsem, device):
        return pltpu.make_async_remote_copy(
            src_ref=src,
            dst_ref=dst,
            send_sem=ssem,
            recv_sem=rsem,
            device_id=device,
            device_id_type=MESH,
        )

    q_to_partner = remote(q_ref, partner_q, psend_sem.at[0], precv_sem.at[0], partner)
    o_to_partner = remote(near_send, partner_o, psend_sem.at[1], precv_sem.at[1], partner)
    s_to_partner = remote(near_stat_send, partner_stat, psend_sem.at[2], precv_sem.at[2], partner)

    def slots_to(peer, mine):
        return remote(
            slots.at[peer], arrived.at[mine], send_sem.at[peer], recv_sem.at[mine], {"seq": peer}
        )

    def out_to(peer, mine):
        return remote(
            ret_send.at[peer], ret.at[mine], osend_sem.at[peer], orecv_sem.at[mine], {"seq": peer}
        )

    def stat_to(peer, mine):
        return remote(
            ret_stat_send.at[peer],
            ret_stat.at[mine],
            ssend_sem.at[peer],
            srecv_sem.at[mine],
            {"seq": peer},
        )

    for table in tables:
        table.wait()
    owners = [owner[r] for r in range(requests)]
    places = []
    for r in range(requests):
        rank = jnp.int32(0)
        for e in range(r):
            rank = rank + jnp.where(owners[e] == owners[r], 1, 0)
        places.append(owners[r] * cap + rank)
    lengths = [suffix_len[r] for r in range(requests)]
    parents = [parent_id[r] for r in range(requests)]

    load_q.wait()

    @pl.when(on_decode)
    def _():
        col = iota((1, tokens), 1)
        target = 2 * spread(col >> 1, places) + (col & 1)
        pick = jnp.where(iota((slot_rows, tokens), 0) == target, 1.0, 0.0).astype(jnp.bfloat16)
        tok = iota((tokens, LANES), 0) >> 1
        pid = spread(tok, parents).astype(jnp.float32).astype(jnp.bfloat16)
        pid_slots = jnp.dot(pick, pid, preferred_element_type=jnp.float32)
        for d in range(n_seq):
            slots[d, :, q_width:] = pid_slots[d * per_peer : (d + 1) * per_peer].astype(
                jnp.bfloat16
            )
        block = 4 * LANES
        for c in range(q_width // block):
            lanes = slice(c * block, (c + 1) * block)
            part = jnp.dot(
                pick, q_ref[:, :, lanes].reshape(tokens, block), preferred_element_type=jnp.float32
            )
            for d in range(n_seq):
                slots[d, :, lanes] = part[d * per_peer : (d + 1) * per_peer].astype(jnp.bfloat16)
        pl.semaphore_wait(barrier, n_seq)
        q_to_partner.start()
        for step in range(n_seq - 1, 0, -1):
            slots_to(peer_at(step), me).start()
        arrived[pl.ds(me, 1)] = slots[pl.ds(me, 1)]

    @pl.when(on_prefill)
    def _():
        pl.semaphore_wait(barrier, 1)

    lane_page = iota((1, key_count), 1) // PAGE
    group_row = jnp.zeros((1, key_count), jnp.int32)
    base_row = jnp.zeros((1, key_count), jnp.int32)
    suf_pages = suffix_pages.shape[0]
    par_pages = parent_pages.shape[1]
    for j in range(key_count // PAGE):
        page = jnp.where(
            on_prefill,
            suffix_pages[j % suf_pages, j // suf_pages],
            parent_pages[j // par_pages, j % par_pages],
        )
        here = lane_page == page
        group_row = jnp.where(here, jnp.where(on_prefill, j // suf_pages, j // par_pages), group_row)
        base_row = jnp.where(
            here, jnp.where(on_prefill, j % suf_pages, j % par_pages) * PAGE, base_row
        )
    pos_row = base_row + (iota((1, key_count), 1) & (PAGE - 1))
    key_meta[0:1, :] = group_row
    key_meta[1:2, :] = pos_row
    load_step.wait()
    for c in range(step_ref.shape[1] // (4 * LANES)):
        lanes = slice(c * 4 * LANES, (c + 1) * 4 * LANES)
        step_ref[:, lanes] = step_in[:, :, lanes].reshape(tokens, 4 * LANES)
    cuts = [parent_len[a] for a in range(parent_len.shape[0])]
    load_kv.wait()

    def attend(get, put, group, limit, step_limit):
        rows = group.shape[0]
        keep = (key_meta[0:1, :] == group) & (key_meta[1:2, :] < limit)
        bias = jnp.where(keep, 0.0, MASKED_SCORE)[None]
        if step_limit is not None:
            step_key = iota((rows, tokens), 1)
            step_keep = ((step_key >> 1) == group) & ((step_key & 1) < step_limit)
            step_bias = jnp.where(step_keep, 0.0, MASKED_SCORE)[None]
        lane = iota((rows, LANES), 1)
        top_all = jnp.zeros((rows, LANES), jnp.float32)
        sum_all = jnp.zeros((rows, LANES), jnp.float32)
        contract = (((1,), (1,)), ((), ()))

        def scores(query, keys, add):
            found = lax.dot_general(query, keys, contract, preferred_element_type=jnp.float32)
            return found.reshape(GROUP, rows, keys.shape[0]) * scale + add

        def blend(term, values):
            term = term.reshape(GROUP * rows, values.shape[0]).astype(jnp.bfloat16)
            mixed = jnp.dot(term, values, preferred_element_type=jnp.float32)
            return mixed.reshape(GROUP, rows, HEAD_DIM)

        for g in range(KV_HEADS):
            query = jnp.concatenate([get(g * GROUP + h) for h in range(GROUP)], axis=0)
            ks = slice(g * HEAD_DIM, (g + 1) * HEAD_DIM)
            vs = slice(key_width + g * HEAD_DIM, key_width + (g + 1) * HEAD_DIM)
            score = scores(query, kv_ref[:, ks], bias)
            top = jnp.max(score, axis=2, keepdims=True)
            if step_limit is not None:
                step_score = scores(query, step_ref[:, ks], step_bias)
                top = jnp.maximum(top, jnp.max(step_score, axis=2, keepdims=True))
            term = jnp.exp(score - top)
            total = jnp.sum(term, axis=2, keepdims=True)
            mixed = blend(term, kv_ref[:, vs])
            if step_limit is not None:
                step_term = jnp.exp(step_score - top)
                total = total + jnp.sum(step_term, axis=2, keepdims=True)
                mixed = mixed + blend(step_term, step_ref[:, vs])
            mixed = mixed / total
            for h in range(GROUP):
                head = g * GROUP + h
                put(head, mixed[h])
                top_all = jnp.where(lane == head, top[h], top_all)
                sum_all = jnp.where(lane == head, total[h], sum_all)
        return top_all, sum_all

    @pl.when(on_prefill)
    def _():
        row = iota((tokens, 1), 0)
        request = row >> 1
        turn = row & 1
        length = spread(request, lengths)

        def lanes_of(head):
            return slice(head * HEAD_DIM, (head + 1) * HEAD_DIM)

        def own(head):
            return q_ref[:, :, lanes_of(head)].reshape(tokens, HEAD_DIM)

        def passed(head):
            return partner_q[:, :, lanes_of(head)].reshape(tokens, HEAD_DIM)

        def serve(head, value):
            out_ref[:, lanes_of(head)] = value.astype(jnp.bfloat16)

        def keep(head, value):
            near_send[:, lanes_of(head)] = value

        q_to_partner.wait_recv()
        top, total = attend(passed, keep, request, length, turn + 1)
        near_stat_send[:, :LANES] = top
        near_stat_send[:, LANES:] = total
        o_to_partner.start()
        s_to_partner.start()
        attend(own, serve, request, length - 1 + turn, None)
        s_to_partner.wait_send()
        o_to_partner.wait_send()

    batch = min(4, n_seq)

    def answer(c):
        steps = [n_seq - 1 - batch * c - i for i in range(batch)]
        peers = [peer_at(step) for step in steps]

        def unless_own(step, action):
            if isinstance(step, int):
                if step > 0:
                    action()
            else:
                pl.when(step > 0)(action)

        for step, peer in zip(steps, peers):
            unless_own(step, lambda peer=peer: slots_to(me, peer).wait_recv())

        def gathered(lanes):
            return jnp.concatenate(
                [arrived[peer, :, lanes].astype(jnp.float32) for peer in peers], axis=0
            )

        def get(head):
            return gathered(slice(head * HEAD_DIM, (head + 1) * HEAD_DIM)).astype(jnp.bfloat16)

        def put(head, value):
            for i, peer in enumerate(peers):
                ret_send[peer, :, head * HEAD_DIM : (head + 1) * HEAD_DIM] = value[
                    i * per_peer : (i + 1) * per_peer
                ].astype(jnp.bfloat16)

        group = gathered(slice(q_width, q_width + LANES)).astype(jnp.int32)[:, 0:1]
        top, total = attend(get, put, group, spread(group, cuts), None)
        for i, peer in enumerate(peers):
            rows = slice(i * per_peer, (i + 1) * per_peer)
            ret_stat_send[peer, :, :LANES] = top[rows]
            ret_stat_send[peer, :, LANES:] = total[rows]

        def reply(peer):
            stat_to(peer, me).start()
            out_to(peer, me).start()

        for step, peer in zip(steps, peers):
            unless_own(step, lambda peer=peer: reply(peer))

    @pl.when(on_decode)
    def _():
        if n_seq // batch <= 4:
            for c in range(n_seq // batch):
                answer(c)
        else:

            def one(c, carry):
                answer(c)
                return carry

            lax.fori_loop(0, n_seq // batch, one, 0)

    @pl.when(on_decode)
    def _():
        ret[pl.ds(me, 1)] = ret_send[pl.ds(me, 1)]
        ret_stat[pl.ds(me, 1)] = ret_stat_send[pl.ds(me, 1)]
        tok = iota((tokens, 1), 0)
        target = 2 * spread(tok >> 1, places) + (tok & 1)
        unpick = jnp.where(iota((tokens, slot_rows), 1) == target, 1.0, 0.0)
        o_to_partner.wait_recv()
        s_to_partner.wait_recv()
        for step in range(n_seq - 1, 0, -1):
            stat_to(me, peer_at(step)).wait_recv()
            out_to(me, peer_at(step)).wait_recv()
        back = jnp.concatenate([ret_stat[s] for s in range(n_seq)], axis=0)
        far = jnp.dot(
            unpick, back, preferred_element_type=jnp.float32, precision=lax.Precision.HIGHEST
        )
        far_top, far_sum = far[:, :LANES], far[:, LANES:]
        near_top, near_sum = partner_stat[:, :LANES], partner_stat[:, LANES:]
        top = jnp.maximum(far_top, near_top)
        far_weight = far_sum * jnp.exp(far_top - top)
        near_weight = near_sum * jnp.exp(near_top - top)
        total = jnp.where(near_weight + far_weight == 0.0, 1.0, near_weight + far_weight)
        far_share = far_weight / total
        near_share = near_weight / total
        unpick = unpick.astype(jnp.bfloat16)
        for head in range(heads_all):
            part = slice(head * HEAD_DIM, (head + 1) * HEAD_DIM)
            came = jnp.concatenate(
                [ret[s, :, part].astype(jnp.float32) for s in range(n_seq)], axis=0
            ).astype(jnp.bfloat16)
            far_out = jnp.dot(unpick, came, preferred_element_type=jnp.float32)
            out_ref[:, part] = (
                far_out * far_share[:, head : head + 1]
                + partner_o[:, part] * near_share[:, head : head + 1]
            ).astype(jnp.bfloat16)
        q_to_partner.wait_send()
        for step in range(1, n_seq):
            peer = peer_at(step)
            slots_to(peer, me).wait_send()
            out_to(peer, me).wait_send()
            stat_to(peer, me).wait_send()


def local(
    kv_store, queries, step_kv, suffix_pages, suffix_len, owner, parent_id, parent_pages, parent_len
):
    n_seq = lax.axis_size("seq")
    page_store = kv_store[0]
    requests, turns, q_width = queries.shape[1:]
    tokens = requests * turns
    cap = max(4, 2 * requests // n_seq)
    per_peer = 2 * cap
    bf16, f32 = jnp.bfloat16, jnp.float32
    vmem = pl.BlockSpec(memory_space=pltpu.VMEM)
    hbm = pl.BlockSpec(memory_space=pl.ANY)
    dma = pltpu.SemaphoreType.DMA
    served = pl.pallas_call(
        functools.partial(kernel, n_seq, cap),
        out_shape=jax.ShapeDtypeStruct((tokens, q_width), bf16),
        in_specs=[hbm] * 9,
        out_specs=vmem,
        scratch_shapes=[
            pltpu.SMEM((requests,), jnp.int32),
            pltpu.SMEM((requests,), jnp.int32),
            pltpu.SMEM((requests,), jnp.int32),
            pltpu.SMEM(suffix_pages.shape[::-1], jnp.int32),
            pltpu.SMEM(parent_pages.shape, jnp.int32),
            pltpu.SMEM(parent_len.shape, jnp.int32),
            pltpu.VMEM((requests, turns, q_width), bf16),
            pltpu.VMEM(page_store.shape, bf16),
            pltpu.VMEM(step_kv.shape, bf16),
            pltpu.VMEM((tokens, step_kv.shape[2]), bf16),
            pltpu.VMEM((n_seq, per_peer, q_width + LANES), bf16),
            pltpu.VMEM((n_seq, per_peer, q_width + LANES), bf16),
            pltpu.VMEM((8, page_store.shape[0]), jnp.int32),
            pltpu.VMEM((tokens, q_width), f32),
            pltpu.VMEM((tokens, 2 * LANES), f32),
            pltpu.VMEM((n_seq, per_peer, q_width), bf16),
            pltpu.VMEM((n_seq, per_peer, 2 * LANES), f32),
            pltpu.VMEM((n_seq, per_peer, q_width), bf16),
            pltpu.VMEM((n_seq, per_peer, 2 * LANES), f32),
            pltpu.VMEM((requests, turns, q_width), bf16),
            pltpu.VMEM((tokens, q_width), f32),
            pltpu.VMEM((tokens, 2 * LANES), f32),
            dma((9,)),
            dma((n_seq,)),
            dma((n_seq,)),
            dma((n_seq,)),
            dma((n_seq,)),
            dma((n_seq,)),
            dma((n_seq,)),
            dma((3,)),
            dma((3,)),
        ],
        compiler_params=pltpu.CompilerParams(
            collective_id=0, has_side_effects=True, vmem_limit_bytes=60 * 1024 * 1024
        ),
    )(
        owner.reshape(-1),
        parent_id,
        suffix_len,
        suffix_pages.T,
        parent_pages,
        parent_len,
        queries[0],
        page_store,
        step_kv,
    )
    return served.reshape(1, requests, turns, q_width)


def solution(mesh):
    in_specs = (
        P("role", ("groups", "seq"), None),
        P("role", ("groups", "seq"), None, None),
        P(("groups", "seq"), None, None),
        P(("groups", "seq"), None),
        P(("groups", "seq")),
        P(("groups", "seq"), None),
        P(("groups", "seq")),
        P(("groups", "seq"), None),
        P(("groups", "seq")),
    )
    out_specs = P("role", ("groups", "seq"), None, None)
    return jax.shard_map(local, mesh=mesh, in_specs=in_specs, out_specs=out_specs, check_vma=False)
```

time: 24.4 us -> 24.5 us (level)
    unnamed x1 -> x0, local copies, waits for them, and re-layouts: 1.85 us -> none
    reshape x0 -> x1, local copies, waits for them, and re-layouts: none -> 1.83 us  [local(): return served.reshape(1, requests, turns, q_width)]
where the time goes in v3:
time: 24.5 us; the launch traced here: 24.4 us
  Pallas kernels  22.5 us (92%)
  local copies, waits for them, and re-layouts  1.83 us (7%)
    pallas_call x1, Pallas kernels, local(): pl.pallas_call(functools.partial(kernel, n_seq, cap), out_shape=jax.Shape...  22.5 us
    reshape x1, local copies, waits for them, and re-layouts, local(): return served.reshape(1, requests, turns, q_width)  1.83 us

profile of v3, /device:TPU:1, one launch (start us, length us, event | category | flops | bytes accessed | tf_op | source)
XLA Modules:
  0.0 24.4 jit_solution(6331157330803012158)
XLA Ops:
  0.0 22.5 %shard_map.91 = bf16[32,4096]{1,0:T(8,128)(2,1)} custom-call(s32[16]{0:T(128)} %bitcast.7, s32[16]{0:T(128)} %parent_id_hbm.1, s32[16]{0:T(128)} %suffix_len_hbm.1, s32[2,16]{1,0:T(2,128)} %bitcast.6, s32[2,16]{1,0:T(2,128)} %parent_pages_hbm.1, s32[2]{0:T(128)} %parent_len_hbm.1, bf16[16,2,4096]{2,1,0:T(2,128)(2,1)} %bitcast.5, bf16[512,1024]{1,0:T(8,128)(2,1)} %bitcast.4, ...), custom_call_target="tpu_custom_call" | custom-call | tf_op jit(solution)/shard_map/pallas_call | solution.py:430
  22.5 1.8 %reshape.7 = bf16[1,16,2,4096]{3,2,1,0:T(2,128)(2,1)} reshape(bf16[32,4096]{1,0:T(8,128)(2,1)} %shard_map.91) | data formatting | bytes 524288 | tf_op jit(solution)/shard_map/reshape | solution.py:482

commit v4 on v3

--- a/solution.py
+++ b/solution.py
@@ -54,6 +54,8 @@
     slots,
     arrived,
     key_meta,
+    slot_bias,
+    far_out,
     near_send,
     near_stat_send,
     ret_send,
@@ -86,6 +88,8 @@
     on_decode = role == 1
     on_prefill = role == 0
     heads_all = KV_HEADS * GROUP
+    group_width = GROUP * HEAD_DIM
+    half = LANES // 2
 
     bits = [(me // 2**b) % 2 for b in range(n_seq.bit_length() - 1)]
 
@@ -147,14 +151,27 @@
     o_to_partner = remote(near_send, partner_o, psend_sem.at[1], precv_sem.at[1], partner)
     s_to_partner = remote(near_stat_send, partner_stat, psend_sem.at[2], precv_sem.at[2], partner)
 
-    def slots_to(peer, mine):
+    def q_lanes(g):
+        first = 0 if g == 0 else LANES + g * group_width
+        return slice(first, LANES + (g + 1) * group_width)
+
+    def slots_to(peer, mine, g):
         return remote(
-            slots.at[peer], arrived.at[mine], send_sem.at[peer], recv_sem.at[mine], {"seq": peer}
-        )
-
-    def out_to(peer, mine):
+            slots.at[peer, :, q_lanes(g)],
+            arrived.at[mine, :, q_lanes(g)],
+            send_sem.at[peer, g],
+            recv_sem.at[mine, g],
+            {"seq": peer},
+        )
+
+    def out_to(peer, mine, g):
+        lanes = slice(g * group_width, (g + 1) * group_width)
         return remote(
-            ret_send.at[peer], ret.at[mine], osend_sem.at[peer], orecv_sem.at[mine], {"seq": peer}
+            ret_send.at[peer, :, lanes],
+            ret.at[mine, :, lanes],
+            osend_sem.at[peer, g],
+            orecv_sem.at[mine, g],
+            {"seq": peer},
         )
 
     def stat_to(peer, mine):
@@ -189,7 +206,7 @@
         pid = spread(tok, parents).astype(jnp.float32).astype(jnp.bfloat16)
         pid_slots = jnp.dot(pick, pid, preferred_element_type=jnp.float32)
         for d in range(n_seq):
-            slots[d, :, q_width:] = pid_slots[d * per_peer : (d + 1) * per_peer].astype(
+            slots[d, :, :LANES] = pid_slots[d * per_peer : (d + 1) * per_peer].astype(
                 jnp.bfloat16
             )
         block = 4 * LANES
@@ -199,11 +216,12 @@
                 pick, q_ref[:, :, lanes].reshape(tokens, block), preferred_element_type=jnp.float32
             )
             for d in range(n_seq):
-                slots[d, :, lanes] = part[d * per_peer : (d + 1) * per_peer].astype(jnp.bfloat16)
+                slots[d, :, LANES + c * block : LANES + (c + 1) * block] = part[d * per_peer : (d + 1) * per_peer].astype(jnp.bfloat16)
         pl.semaphore_wait(barrier, n_seq)
         q_to_partner.start()
-        for step in range(n_seq - 1, 0, -1):
-            slots_to(peer_at(step), me).start()
+        for g in range(KV_HEADS):
+            for step in range(n_seq - 1, 0, -1):
+                slots_to(peer_at(step), me, g).start()
         arrived[pl.ds(me, 1)] = slots[pl.ds(me, 1)]
 
     @pl.when(on_prefill)
@@ -236,51 +254,49 @@
     cuts = [parent_len[a] for a in range(parent_len.shape[0])]
     load_kv.wait()
 
-    def attend(get, put, group, limit, step_limit):
-        rows = group.shape[0]
+    def bias_of(group, limit):
         keep = (key_meta[0:1, :] == group) & (key_meta[1:2, :] < limit)
-        bias = jnp.where(keep, 0.0, MASKED_SCORE)[None]
-        if step_limit is not None:
-            step_key = iota((rows, tokens), 1)
-            step_keep = ((step_key >> 1) == group) & ((step_key & 1) < step_limit)
-            step_bias = jnp.where(step_keep, 0.0, MASKED_SCORE)[None]
-        lane = iota((rows, LANES), 1)
-        top_all = jnp.zeros((rows, LANES), jnp.float32)
-        sum_all = jnp.zeros((rows, LANES), jnp.float32)
+        return jnp.where(keep, 0.0, MASKED_SCORE)
+
+    def attend(g, query, bias, step_bias=None):
+        rows = bias.shape[0]
+        ks = slice(g * HEAD_DIM, (g + 1) * HEAD_DIM)
+        vs = slice(key_width + g * HEAD_DIM, key_width + (g + 1) * HEAD_DIM)
         contract = (((1,), (1,)), ((), ()))
 
-        def scores(query, keys, add):
+        def scores(keys, add):
             found = lax.dot_general(query, keys, contract, preferred_element_type=jnp.float32)
-            return found.reshape(GROUP, rows, keys.shape[0]) * scale + add
+            return found.reshape(GROUP, rows, keys.shape[0]) * scale + add[None]
 
         def blend(term, values):
             term = term.reshape(GROUP * rows, values.shape[0]).astype(jnp.bfloat16)
             mixed = jnp.dot(term, values, preferred_element_type=jnp.float32)
             return mixed.reshape(GROUP, rows, HEAD_DIM)
 
-        for g in range(KV_HEADS):
-            query = jnp.concatenate([get(g * GROUP + h) for h in range(GROUP)], axis=0)
-            ks = slice(g * HEAD_DIM, (g + 1) * HEAD_DIM)
-            vs = slice(key_width + g * HEAD_DIM, key_width + (g + 1) * HEAD_DIM)
-            score = scores(query, kv_ref[:, ks], bias)
-            top = jnp.max(score, axis=2, keepdims=True)
-            if step_limit is not None:
-                step_score = scores(query, step_ref[:, ks], step_bias)
-                top = jnp.maximum(top, jnp.max(step_score, axis=2, keepdims=True))
-            term = jnp.exp(score - top)
-            total = jnp.sum(term, axis=2, keepdims=True)
-            mixed = blend(term, kv_ref[:, vs])
-            if step_limit is not None:
-                step_term = jnp.exp(step_score - top)
-                total = total + jnp.sum(step_term, axis=2, keepdims=True)
-                mixed = mixed + blend(step_term, step_ref[:, vs])
-            mixed = mixed / total
-            for h in range(GROUP):
-                head = g * GROUP + h
-                put(head, mixed[h])
-                top_all = jnp.where(lane == head, top[h], top_all)
-                sum_all = jnp.where(lane == head, total[h], sum_all)
-        return top_all, sum_all
+        score = scores(kv_ref[:, ks], bias)
+        top = jnp.max(score, axis=2, keepdims=True)
+        if step_bias is not None:
+            step_score = scores(step_ref[:, ks], step_bias)
+            top = jnp.maximum(top, jnp.max(step_score, axis=2, keepdims=True))
+        term = jnp.exp(score - top)
+        total = jnp.sum(term, axis=2, keepdims=True)
+        mixed = blend(term, kv_ref[:, vs])
+        if step_bias is not None:
+            step_term = jnp.exp(step_score - top)
+            total = total + jnp.sum(step_term, axis=2, keepdims=True)
+            mixed = mixed + blend(step_term, step_ref[:, vs])
+        return mixed / total, top, total
+
+    def record(g, top, total):
+        lane = iota((top.shape[1], LANES), 1)
+        stat = jnp.zeros(lane.shape, jnp.float32)
+        for h in range(GROUP):
+            stat = jnp.where(lane == g * GROUP + h, top[h], stat)
+            stat = jnp.where(lane == half + g * GROUP + h, total[h], stat)
+        return stat
+
+    def swapped(stat):
+        return jnp.concatenate([stat[:, half:], stat[:, :half]], axis=1)
 
     @pl.when(on_prefill)
     def _():
@@ -305,18 +321,35 @@
             near_send[:, lanes_of(head)] = value
 
         q_to_partner.wait_recv()
-        top, total = attend(passed, keep, request, length, turn + 1)
-        near_stat_send[:, :LANES] = top
-        near_stat_send[:, LANES:] = total
+        bias = bias_of(request, length)
+        step_key = iota((tokens, tokens), 1)
+        step_keep = ((step_key >> 1) == request) & ((step_key & 1) < turn + 1)
+        step_bias = jnp.where(step_keep, 0.0, MASKED_SCORE)
+        stat = jnp.zeros((tokens, LANES), jnp.float32)
+        for g in range(KV_HEADS):
+            heads = range(g * GROUP, (g + 1) * GROUP)
+            query = jnp.concatenate([passed(head) for head in heads], axis=0)
+            mixed, top, total = attend(g, query, bias, step_bias)
+            for h, head in enumerate(heads):
+                keep(head, mixed[h])
+            stat = stat + record(g, top, total)
+        near_stat_send[...] = stat
         o_to_partner.start()
         s_to_partner.start()
-        attend(own, serve, request, length - 1 + turn, None)
+        bias = bias_of(request, length - 1 + turn)
+        for g in range(KV_HEADS):
+            heads = range(g * GROUP, (g + 1) * GROUP)
+            query = jnp.concatenate([own(head) for head in heads], axis=0)
+            mixed, _, _ = attend(g, query, bias)
+            for h, head in enumerate(heads):
+                serve(head, mixed[h])
         s_to_partner.wait_send()
         o_to_partner.wait_send()
 
-    batch = min(4, n_seq)
-
-    def answer(c):
+    batch = min(8, n_seq)
+    batch_rows = batch * per_peer
+
+    def answer(c, g):
         steps = [n_seq - 1 - batch * c - i for i in range(batch)]
         peers = [peer_at(step) for step in steps]
 
@@ -328,48 +361,57 @@
                 pl.when(step > 0)(action)
 
         for step, peer in zip(steps, peers):
-            unless_own(step, lambda peer=peer: slots_to(me, peer).wait_recv())
-
-        def gathered(lanes):
+            unless_own(step, lambda peer=peer: slots_to(me, peer, g).wait_recv())
+
+        def gathered(first):
             return jnp.concatenate(
-                [arrived[peer, :, lanes].astype(jnp.float32) for peer in peers], axis=0
+                [arrived[peer, :, first : first + LANES].astype(jnp.float32) for peer in peers],
+                axis=0,
             )
 
-        def get(head):
-            return gathered(slice(head * HEAD_DIM, (head + 1) * HEAD_DIM)).astype(jnp.bfloat16)
-
-        def put(head, value):
+        rows = pl.ds(c * batch_rows, batch_rows)
+        if g == 0:
+            group = gathered(0).astype(jnp.int32)[:, 0:1]
+            slot_bias[rows, :] = bias_of(group, spread(group, cuts))
+        query = jnp.concatenate(
+            [
+                gathered(LANES + head * HEAD_DIM).astype(jnp.bfloat16)
+                for head in range(g * GROUP, (g + 1) * GROUP)
+            ],
+            axis=0,
+        )
+        mixed, top, total = attend(g, query, slot_bias[rows, :])
+        for h in range(GROUP):
+            head = g * GROUP + h
             for i, peer in enumerate(peers):
-                ret_send[peer, :, head * HEAD_DIM : (head + 1) * HEAD_DIM] = value[
-                    i * per_peer : (i + 1) * per_peer
+                ret_send[peer, :, head * HEAD_DIM : (head + 1) * HEAD_DIM] = mixed[
+                    h, i * per_peer : (i + 1) * per_peer
                 ].astype(jnp.bfloat16)
-
-        group = gathered(slice(q_width, q_width + LANES)).astype(jnp.int32)[:, 0:1]
-        top, total = attend(get, put, group, spread(group, cuts), None)
+        stat = record(g, top, total)
         for i, peer in enumerate(peers):
-            rows = slice(i * per_peer, (i + 1) * per_peer)
-            ret_stat_send[peer, :, :LANES] = top[rows]
-            ret_stat_send[peer, :, LANES:] = total[rows]
+            part = stat[i * per_peer : (i + 1) * per_peer]
+            ret_stat_send[peer] = part if g == 0 else ret_stat_send[peer] + part
 
         def reply(peer):
-            stat_to(peer, me).start()
-            out_to(peer, me).start()
+            if g == KV_HEADS - 1:
+                stat_to(peer, me).start()
+            out_to(peer, me, g).start()
 
         for step, peer in zip(steps, peers):
             unless_own(step, lambda peer=peer: reply(peer))
 
     @pl.when(on_decode)
     def _():
-        if n_seq // batch <= 4:
-            for c in range(n_seq // batch):
-                answer(c)
-        else:
-
-            def one(c, carry):
-                answer(c)
-                return carry
-
-            lax.fori_loop(0, n_seq // batch, one, 0)
+        for g in range(KV_HEADS):
+            if n_seq == batch:
+                answer(0, g)
+            else:
+
+                def one(c, carry):
+                    answer(c, g)
+                    return carry
+
+                lax.fori_loop(0, n_seq // batch, one, 0)
 
     @pl.when(on_decode)
     def _():
@@ -380,37 +422,43 @@
         unpick = jnp.where(iota((tokens, slot_rows), 1) == target, 1.0, 0.0)
         o_to_partner.wait_recv()
         s_to_partner.wait_recv()
+        pick_back = unpick.astype(jnp.bfloat16)
+        for g in range(KV_HEADS):
+            for step in range(n_seq - 1, 0, -1):
+                out_to(me, peer_at(step), g).wait_recv()
+            for head in range(g * GROUP, (g + 1) * GROUP):
+                part = slice(head * HEAD_DIM, (head + 1) * HEAD_DIM)
+                came = jnp.concatenate(
+                    [ret[s, :, part].astype(jnp.float32) for s in range(n_seq)], axis=0
+                ).astype(jnp.bfloat16)
+                far_out[:, part] = jnp.dot(pick_back, came, preferred_element_type=jnp.float32)
         for step in range(n_seq - 1, 0, -1):
             stat_to(me, peer_at(step)).wait_recv()
-            out_to(me, peer_at(step)).wait_recv()
         back = jnp.concatenate([ret_stat[s] for s in range(n_seq)], axis=0)
-        far = jnp.dot(
+        far_top = jnp.dot(
             unpick, back, preferred_element_type=jnp.float32, precision=lax.Precision.HIGHEST
         )
-        far_top, far_sum = far[:, :LANES], far[:, LANES:]
-        near_top, near_sum = partner_stat[:, :LANES], partner_stat[:, LANES:]
+        far_sum = swapped(far_top)
+        near_top = partner_stat[...]
+        near_sum = swapped(near_top)
         top = jnp.maximum(far_top, near_top)
         far_weight = far_sum * jnp.exp(far_top - top)
         near_weight = near_sum * jnp.exp(near_top - top)
         total = jnp.where(near_weight + far_weight == 0.0, 1.0, near_weight + far_weight)
         far_share = far_weight / total
         near_share = near_weight / total
-        unpick = unpick.astype(jnp.bfloat16)
         for head in range(heads_all):
             part = slice(head * HEAD_DIM, (head + 1) * HEAD_DIM)
-            came = jnp.concatenate(
-                [ret[s, :, part].astype(jnp.float32) for s in range(n_seq)], axis=0
-            ).astype(jnp.bfloat16)
-            far_out = jnp.dot(unpick, came, preferred_element_type=jnp.float32)
             out_ref[:, part] = (
-                far_out * far_share[:, head : head + 1]
+                far_out[:, part] * far_share[:, head : head + 1]
                 + partner_o[:, part] * near_share[:, head : head + 1]
             ).astype(jnp.bfloat16)
         q_to_partner.wait_send()
         for step in range(1, n_seq):
             peer = peer_at(step)
-            slots_to(peer, me).wait_send()
-            out_to(peer, me).wait_send()
+            for g in range(KV_HEADS):
+                slots_to(peer, me, g).wait_send()
+                out_to(peer, me, g).wait_send()
             stat_to(peer, me).wait_send()
 
 
@@ -446,20 +494,22 @@
             pltpu.VMEM((n_seq, per_peer, q_width + LANES), bf16),
             pltpu.VMEM((n_seq, per_peer, q_width + LANES), bf16),
             pltpu.VMEM((8, page_store.shape[0]), jnp.int32),
+            pltpu.VMEM((n_seq * per_peer, page_store.shape[0]), f32),
             pltpu.VMEM((tokens, q_width), f32),
-            pltpu.VMEM((tokens, 2 * LANES), f32),
+            pltpu.VMEM((tokens, q_width), f32),
+            pltpu.VMEM((tokens, LANES), f32),
             pltpu.VMEM((n_seq, per_peer, q_width), bf16),
-            pltpu.VMEM((n_seq, per_peer, 2 * LANES), f32),
+            pltpu.VMEM((n_seq, per_peer, LANES), f32),
             pltpu.VMEM((n_seq, per_peer, q_width), bf16),
-            pltpu.VMEM((n_seq, per_peer, 2 * LANES), f32),
+            pltpu.VMEM((n_seq, per_peer, LANES), f32),
             pltpu.VMEM((requests, turns, q_width), bf16),
             pltpu.VMEM((tokens, q_width), f32),
-            pltpu.VMEM((tokens, 2 * LANES), f32),
+            pltpu.VMEM((tokens, LANES), f32),
             dma((9,)),
-            dma((n_seq,)),
-            dma((n_seq,)),
-            dma((n_seq,)),
-            dma((n_seq,)),
+            dma((n_seq, KV_HEADS)),
+            dma((n_seq, KV_HEADS)),
+            dma((n_seq, KV_HEADS)),
+            dma((n_seq, KV_HEADS)),
             dma((n_seq,)),
             dma((n_seq,)),
             dma((3,)),

time: 24.5 us -> 23.2 us (0.947)
  Pallas kernels: 22.5 us -> 21.2 us
    pallas_call x1, Pallas kernels: 22.5 us -> 21.2 us  [local(): pl.pallas_call(functools.partial(kernel, n_seq, cap), out_shape=jax.Shape...]
where the time goes in v4:
time: 23.2 us; the launch traced here: 23 us
  Pallas kernels  21.2 us (91%)
  local copies, waits for them, and re-layouts  1.83 us (8%)
    pallas_call x1, Pallas kernels, local(): pl.pallas_call(functools.partial(kernel, n_seq, cap), out_shape=jax.Shape...  21.2 us
    reshape x1, local copies, waits for them, and re-layouts, local(): return served.reshape(1, requests, turns, q_width)  1.83 us

profile of v4, /device:TPU:1, one launch (start us, length us, event | category | flops | bytes accessed | tf_op | source)
XLA Modules:
  0.0 23.0 jit_solution(14348993815142706352)
XLA Ops:
  0.0 21.2 %shard_map.91 = bf16[32,4096]{1,0:T(8,128)(2,1)} custom-call(s32[16]{0:T(128)} %bitcast.7, s32[16]{0:T(128)} %parent_id_hbm.1, s32[16]{0:T(128)} %suffix_len_hbm.1, s32[2,16]{1,0:T(2,128)} %bitcast.6, s32[2,16]{1,0:T(2,128)} %parent_pages_hbm.1, s32[2]{0:T(128)} %parent_len_hbm.1, bf16[16,2,4096]{2,1,0:T(2,128)(2,1)} %bitcast.5, bf16[512,1024]{1,0:T(8,128)(2,1)} %bitcast.4, ...), custom_call_target="tpu_custom_call" | custom-call | tf_op jit(solution)/shard_map/pallas_call | solution.py:478
  21.2 1.8 %reshape.7 = bf16[1,16,2,4096]{3,2,1,0:T(2,128)(2,1)} reshape(bf16[32,4096]{1,0:T(8,128)(2,1)} %shard_map.91) | data formatting | bytes 524288 | tf_op jit(solution)/shard_map/reshape | solution.py:532

commit v5 on v4

--- a/solution.py
+++ b/solution.py
@@ -105,6 +105,16 @@
                 peer = peer + 2**b * (1 - 2 * mine) * ((step // 2**b) % 2)
         return peer
 
+    barrier = pltpu.get_barrier_semaphore()
+    @pl.when(on_decode)
+    def _():
+        for step in range(n_seq - 1, 0, -1):
+            pl.semaphore_signal(
+                barrier, inc=1, device_id={"seq": peer_at(step)}, device_id_type=MESH
+            )
+
+    pl.semaphore_signal(barrier, inc=1, device_id=partner, device_id_type=MESH)
+
     load_q = pltpu.make_async_copy(q_hbm, q_ref, load_sem.at[0])
     load_step = pltpu.make_async_copy(step_hbm, step_in, load_sem.at[1])
     load_kv = pltpu.make_async_copy(kv_hbm, kv_ref, load_sem.at[2])
@@ -126,16 +136,6 @@
         table.start()
     load_step.start()
     load_kv.start()
-
-    barrier = pltpu.get_barrier_semaphore()
-    pl.semaphore_signal(barrier, inc=1, device_id=partner, device_id_type=MESH)
-
-    @pl.when(on_decode)
-    def _():
-        for step in range(1, n_seq):
-            pl.semaphore_signal(
-                barrier, inc=1, device_id={"seq": peer_at(step)}, device_id_type=MESH
-            )
 
     def remote(src, dst, ssem, rsem, device):
         return pltpu.make_async_remote_copy(
@@ -446,12 +446,11 @@
         near_weight = near_sum * jnp.exp(near_top - top)
         total = jnp.where(near_weight + far_weight == 0.0, 1.0, near_weight + far_weight)
         far_share = far_weight / total
-        near_share = near_weight / total
         for head in range(heads_all):
             part = slice(head * HEAD_DIM, (head + 1) * HEAD_DIM)
+            near = partner_o[:, part]
             out_ref[:, part] = (
-                far_out[:, part] * far_share[:, head : head + 1]
-                + partner_o[:, part] * near_share[:, head : head + 1]
+                near + (far_out[:, part] - near) * far_share[:, head : head + 1]
             ).astype(jnp.bfloat16)
         q_to_partner.wait_send()
         for step in range(1, n_seq):
@@ -477,7 +476,7 @@
     dma = pltpu.SemaphoreType.DMA
     served = pl.pallas_call(
         functools.partial(kernel, n_seq, cap),
-        out_shape=jax.ShapeDtypeStruct((tokens, q_width), bf16),
+        out_shape=pltpu.VMEM((tokens, q_width), bf16),
         in_specs=[hbm] * 9,
         out_specs=vmem,
         scratch_shapes=[

time: 23.2 us -> 21.4 us (0.922)
  local copies, waits for them, and re-layouts: 1.83 us -> 0.89 us
  Pallas kernels: 21.2 us -> 20.3 us
    reshape x1, local copies, waits for them, and re-layouts: 1.83 us -> 0.89 us  [local(): return served.reshape(1, requests, turns, q_width)]
    pallas_call x1, Pallas kernels: 21.2 us -> 20.3 us  [local(): pl.pallas_call(functools.partial(kernel, n_seq, cap), out_shape=pltpu.VME...]
where the time goes in v5:
time: 21.4 us; the launch traced here: 21.2 us
  Pallas kernels  20.3 us (95%)
  local copies, waits for them, and re-layouts  0.89 us (4%)
    pallas_call x1, Pallas kernels, local(): pl.pallas_call(functools.partial(kernel, n_seq, cap), out_shape=pltpu.VME...  20.3 us
    reshape x1, local copies, waits for them, and re-layouts, local(): return served.reshape(1, requests, turns, q_width)  0.89 us

profile of v5, /device:TPU:1, one launch (start us, length us, event | category | flops | bytes accessed | tf_op | source)
XLA Modules:
  0.0 21.2 jit_solution(10218146186263559846)
XLA Ops:
  0.0 20.3 %shard_map.91 = bf16[32,4096]{1,0:T(8,128)(2,1)S(1)} custom-call(s32[16]{0:T(128)} %bitcast.7, s32[16]{0:T(128)} %parent_id_hbm.1, s32[16]{0:T(128)} %suffix_len_hbm.1, s32[2,16]{1,0:T(2,128)} %bitcast.6, s32[2,16]{1,0:T(2,128)} %parent_pages_hbm.1, s32[2]{0:T(128)} %parent_len_hbm.1, bf16[16,2,4096]{2,1,0:T(2,128)(2,1)} %bitcast.5, ...), custom_call_target="tpu_custom_call" | custom-call | tf_op jit(solution)/shard_map/pallas_call | solution.py:477
  20.3 0.9 %reshape.7 = bf16[1,16,2,4096]{3,2,1,0:T(2,128)(2,1)} reshape(bf16[32,4096]{1,0:T(8,128)(2,1)S(1)} %shard_map.91) | data formatting | bytes 524288 | tf_op jit(solution)/shard_map/reshape | solution.py:531
